TPU v7x, 256 devices: a whole 4x4x8 slice. The times are simulated.
256 devices in a mesh: tile: 64 (over y, x, z_lo), rep: 4 (over z_hi, core).
Axes of the slice: x: 4, y: 4, z: 8 (z_hi: 2, z_lo: 4; z = z_hi * 4 + z_lo), core: 2. Of those that a mesh axis runs over, the one named last changes fastest.
Arguments:
- inputs: bfloat16 [65536, 1024], P(('rep', 'tile')), parts along dimension 0, may hold values from -6 to 6
- queries: bfloat16 [65536, 1024], P(('rep', 'tile')), parts along dimension 0, may hold values from -180 to 180
- key_vectors: bfloat16 [65536, 1024], P(('rep', 'tile')), parts along dimension 0, may hold values from -6 to 6
- values: bfloat16 [65536, 1024], P(('rep', 'tile')), parts along dimension 0, may hold values from -16 to 16
- out_weight: bfloat16 [1024, 1024], replicated, may hold values from -0.1875 to 0.1875
- norm_gain: float32 [1024], replicated, may hold values from 0.5 to 1.5
- routes: int32 [65536, 2], P(('rep', 'tile')), parts along dimension 0, may hold values from 0 to 63, all different within a row; in each aligned block of 128 rows (0 to 127, 128 to 255, ...) at most 8 rows name the same one
- route_gates: float32 [65536, 2], P(('rep', 'tile')), parts along dimension 0, may hold values from 0.2 to 1
- w_gate: bfloat16 [64, 1024, 1408], P('tile'), may hold values from -0.1875 to 0.1875
- w_up: bfloat16 [64, 1024, 1408], P('tile'), may hold values from -0.1875 to 0.1875
- w_down: bfloat16 [64, 1408, 1024], P('tile'), may hold values from -0.15625 to 0.15625
Outputs:
- layer_out: bfloat16 [65536, 1024], P(('rep', 'tile')), parts along dimension 0
There are 4 independent parts, one for each index of `rep`. A program takes and returns all parts, laid end to end along the dimension named above; an argument that names none is the same for every part. Nothing has to cross between parts.
Inputs may be any that keep to these rules, and one draw needn't show every extreme that they name: `routes`: in each aligned block of 128 tokens no expert is named by more than 8 tokens, and some expert is named by exactly that many; each token names 2 different experts.
All inputs are finite; a program needn't handle non-finite values.
Results may differ from a plain program's by a relative error of at most 0.0061.
Values may be sent and summed in bfloat16 or wider, within the bound.
A program may use at most 64 MiB of HBM per device.

v0:
```python
import jax
import jax.numpy as jnp
from jax import lax
from jax.sharding import PartitionSpec as P

HEADS = 16
HD = 64
IL_DEV = 4
XL = 8
DP = 8
R_IL = 2
R_XL = 2
R_DP = 2


def with_halo(shard, sides, width):
    for axis, dim in sides:
        count, length = (lax.axis_size(axis), shard.shape[dim])
        up = [(i, (i + 1) % count) for i in range(count - 1)]
        down = [(j, i) for i, j in up]
        last = lax.slice_in_dim(shard, length - width, length, axis=dim)
        initial = lax.slice_in_dim(shard, 0, width, axis=dim)
        before = lax.ppermute(last, axis, up)
        after = lax.ppermute(initial, axis, down)
        shard = jnp.concatenate([before, shard, after], axis=dim)
    return shard


def local_attention(query_block, key_block, value_block, first_inline, total_inlines):
    query_count = query_block.shape[0]
    key_count = key_block.shape[0]
    plane = XL * DP
    query_pos = jnp.arange(query_count, dtype=jnp.int32)
    key_pos = jnp.arange(key_count, dtype=jnp.int32)
    query_il = query_pos // plane
    query_xl = query_pos // DP % XL
    query_dp = query_pos % DP
    key_il = key_pos // plane - R_IL
    key_xl = key_pos // DP % XL
    key_dp = key_pos % DP
    near = jnp.abs(query_il[:, None] - key_il[None, :]) <= R_IL
    near = near & (jnp.abs(query_xl[:, None] - key_xl[None, :]) <= R_XL)
    near = near & (jnp.abs(query_dp[:, None] - key_dp[None, :]) <= R_DP)
    inside = (first_inline + key_il >= 0) & (first_inline + key_il < total_inlines)
    near = near & inside[None, :]
    query_heads = query_block.reshape(query_count, HEADS, HD)
    key_heads = key_block.reshape(key_count, HEADS, HD)
    value_heads = value_block.reshape(key_count, HEADS, HD)
    scores = jnp.einsum(
        "qhd,khd->hqk", query_heads, key_heads, preferred_element_type=jnp.float32
    ) * (1.0 / HD**0.5)
    scores = jnp.where(near[None], scores, jnp.float32(-1e30))
    highest = jnp.max(scores, axis=-1, keepdims=True)
    weights = jnp.exp(scores - highest)
    weights = jnp.where(near[None], weights, jnp.float32(0.0))
    totals = jnp.sum(weights, axis=-1, keepdims=True)
    probs = (weights / totals).astype(jnp.bfloat16)
    attended = jnp.einsum("hqk,khd->qhd", probs, value_heads, preferred_element_type=jnp.float32)
    return attended.astype(jnp.bfloat16).reshape(query_count, HEADS * HD)


def expert_rows(token_rows, gate_mat, up_mat, down_mat):
    gate_part = jnp.dot(token_rows, gate_mat, preferred_element_type=jnp.float32)
    up_part = jnp.dot(token_rows, up_mat, preferred_element_type=jnp.float32)
    hidden = (jax.nn.silu(gate_part) * up_part).astype(jnp.bfloat16)
    return jnp.dot(hidden, down_mat, preferred_element_type=jnp.float32).astype(jnp.bfloat16)


def slot_ranks(routes, experts, block_rows):
    row_count = routes.shape[0]
    expert_ids = jnp.arange(experts, dtype=jnp.int32)
    matches = routes[:, :, None] == expert_ids[None, None, :]
    hits = jnp.sum(matches.astype(jnp.int32), axis=1)
    hits = hits.reshape(row_count // block_rows, block_rows, experts)
    earlier = (jnp.cumsum(hits, axis=1) - hits).reshape(row_count, experts)
    return jnp.sum(jnp.where(matches, earlier[:, None, :], 0), axis=-1)


def local(
    inputs,
    queries,
    key_vectors,
    values,
    out_weight,
    norm_gain,
    routes,
    route_gates,
    w_gate,
    w_up,
    w_down,
):
    row_count = inputs.shape[0]
    model = inputs.shape[1]
    tiles = lax.axis_size("tile")
    first_inline = lax.axis_index("tile") * IL_DEV
    width = R_IL * XL * DP
    key_value = jnp.concatenate([key_vectors, values], axis=1)
    extended = with_halo(key_value, (("tile", 0),), width)
    attended = local_attention(
        queries, extended[:, :model], extended[:, model:], first_inline, IL_DEV * tiles
    )
    residual = (
        inputs.astype(jnp.float32)
        + jnp.dot(attended, out_weight, preferred_element_type=jnp.float32)
    ).astype(jnp.bfloat16)
    resid_float = residual.astype(jnp.float32)
    mean_square = jnp.mean(resid_float * resid_float, axis=-1, keepdims=True)
    normed = (resid_float * lax.rsqrt(mean_square + 1e-06) * norm_gain[None, :]).astype(
        jnp.bfloat16
    )
    route_width = routes.shape[1]
    block_rows = row_count // 2
    capacity = row_count * route_width // tiles
    slot_rank = slot_ranks(routes, tiles, block_rows)
    gate_mat = w_gate[0]
    up_mat = w_up[0]
    down_mat = w_down[0]
    half_index = (jnp.arange(row_count, dtype=jnp.int32) // block_rows)[:, None]
    positions = routes * (2 * capacity) + half_index * capacity + slot_rank
    copies = jnp.broadcast_to(normed[:, None, :], (row_count, route_width, model)).reshape(
        -1, model
    )
    outgoing = (
        jnp.zeros((tiles * 2 * capacity, model), jnp.bfloat16).at[positions.reshape(-1)].set(copies)
    )
    outgoing = outgoing.reshape(tiles, 2 * capacity, model)
    received = lax.all_to_all(outgoing, "tile", split_axis=0, concat_axis=0, tiled=True)
    produced = expert_rows(received.reshape(-1, model), gate_mat, up_mat, down_mat).reshape(
        received.shape
    )
    returned = lax.all_to_all(produced, "tile", split_axis=0, concat_axis=0, tiled=True)
    picked = returned.reshape(-1, model)[positions]
    combined = jnp.sum(route_gates[:, :, None] * picked.astype(jnp.float32), axis=1)
    return (resid_float + combined).astype(jnp.bfloat16)


def solution(mesh):
    return jax.shard_map(
        local,
        mesh=mesh,
        in_specs=(
            P(("rep", "tile"), None),
            P(("rep", "tile"), None),
            P(("rep", "tile"), None),
            P(("rep", "tile"), None),
            P(),
            P(),
            P(("rep", "tile"), None),
            P(("rep", "tile"), None),
            P("tile", None, None),
            P("tile", None, None),
            P("tile", None, None),
        ),
        out_specs=P(("rep", "tile"), None),
        check_vma=False,
    )
```

profile of v0, /device:TPU:64, one launch (start us, length us, event | category | flops | bytes accessed | tf_op | source)
XLA Modules:
  0.0 210.8 jit_solution(6665938544974771941)
XLA Ops:
  0.0 0.0 copy-start
  0.0 0.0 copy-start.4
  0.0 0.0 copy-start.7
  0.0 1.2 constant_dynamic-update-slice_fusion.1
  1.2 1.1 constant_dynamic-update-slice_fusion
  2.3 0.0 copy-start.1
  2.3 1.0 copy-done.1
  3.3 1.1 fusion.47
  4.4 3.8 %collective-permute-start = (bf16[128,2048]{1,0:T(8,128)(2,1)}, bf16[128,2048]{1,0:T(8,128)(2,1)}, u32[]{:S(2)}, u32[]{:S(2)}) collective-permute-start(bf16[128,2048]{1,0:T(8,128)(2,1)} %get-tuple-element.9), channel_id=1, source_target_pairs={{0,4},{4,8},{8,12},{12,16},{16,20},{20,24},{24,28},{28,32},{32,36}... | collective-permute-start | bytes 1572872 | tf_op jit(solution)/shard_map/ppermute | solution.py:23
  8.2 2.0 collective-permute-start.1
  10.2 0.6 and_select_fusion.1
  10.8 0.6 and_select_fusion.4
  11.4 0.0 copy-done.4
  11.4 1.0 copy.28
  12.4 0.0 copy-done.7
  12.5 0.1 copy.36
  12.5 0.2 reduce_window_sum.13
  12.7 0.1 copy.32
  12.9 0.1 copy.33
  13.0 0.1 reshape.300
  13.2 0.6 compare_select_fusion
  13.8 1.1 fusion.30
  14.9 5.3 %collective-permute-done = bf16[128,2048]{1,0:T(8,128)(2,1)} collective-permute-done((bf16[128,2048]{1,0:T(8,128)(2,1)}, bf16[128,2048]{1,0:T(8,128)(2,1)}, u32[]{:S(2)}, u32[]{:S(2)}) %collective-permute-start) | collective-permute-done | bytes 524320 | tf_op jit(solution)/shard_map/ppermute | solution.py:23
  20.2 11.5 %collective-permute-done.1 = bf16[128,2048]{1,0:T(8,128)(2,1)} collective-permute-done((bf16[128,2048]{1,0:T(8,128)(2,1)}, bf16[128,2048]{1,0:T(8,128)(2,1)}, u32[]{:S(2)}, u32[]{:S(2)}) %collective-permute-start.1) | collective-permute-done | bytes 524320 | tf_op jit(solution)/shard_map/ppermute | solution.py:24
  31.7 1.7 pad_maximum_fusion
  33.4 1.6 fusion.46
  34.9 0.0 copy-start.5
  34.9 2.4 %copy.27 = bf16[512,1024]{0,1:T(8,128)(2,1)} copy(bf16[512,1024]{1,0:T(8,128)(2,1)} %get-tuple-element.7) | data formatting | bytes 2097152 | tf_op jit(solution)/shard_map/slice | solution.py:100
  37.3 2.3 %copy.26 = bf16[512,1024]{0,1:T(8,128)(2,1)} copy(bf16[512,1024]{1,0:T(8,128)(2,1)} %get-tuple-element.8) | data formatting | bytes 2097152 | tf_op jit(solution)/shard_map/slice | solution.py:100
  39.6 0.0 copy-done.5
  39.6 8.4 %fusion.48 = (f32[16,256]{1,0:T(8,128)}, f32[16,256,512]{1,2,0:T(8,128)}) fusion(pred[256,512]{0,1:T(8,128)(4,1)S(1)} %fusion.30, bf16[512,16,64]{0,2,1:T(8,128)(2,1)} %bitcast.52, bf16[256,16,64]{0,2,1:T(8,128)(2,1)S(1)} %bitcast.54), kind=kOutput, calls=%fused_computation.92 | convolution fusion | flops 278921728 | bytes 10108928 | tf_op jit(solution)/shard_map/sub | solution.py:54
  48.0 0.0 copy-start.2
  48.0 0.0 copy-start.6
  48.0 4.6 %fusion.18 = bf16[16,64,256]{2,1,0:T(8,128)(2,1)S(1)} fusion(bf16[512,16,64]{0,2,1:T(8,128)(2,1)} %bitcast.53, f32[16,256,512]{1,2,0:T(8,128)} %get-tuple-element.12, f32[16,256]{1,0:T(8,128)} %get-tuple-element.11), kind=kOutput, calls=%fused_computation.24 | convolution fusion | flops 272891904 | bytes 9977856 | tf_op jit(solution)/shard_map/hqk,khd->qhd/dot_general | solution.py:58
  52.6 0.0 copy-start.8
  52.6 0.0 copy-done.2
  52.6 0.0 copy-done.6
  52.7 0.8 fusion.20
  53.5 0.0 copy-done.8
  53.5 0.2 fusion.22
  53.7 1.5 broadcast_in_dim.66
  55.3 2.3 %reshape.318 = bf16[512,1024]{1,0:T(8,128)(2,1)} reshape(bf16[256,2,1024]{2,1,0:T(2,128)(2,1)} %broadcast_in_dim.66) | data formatting | bytes 2097152 | tf_op jit(solution)/shard_map/reshape | solution.py:120
  57.5 4.8 %scatter_custom_fusion = bf16[1024,1024]{1,0:T(8,128)(2,1)} fusion(s32[512]{0:T(512)} %bitcast.58, bf16[512,1024]{1,0:T(8,128)(2,1)} %reshape.318, bf16[]{:T(256)} %constant.135.clone.1), kind=kCustom, calls=%fused_computation.30 | custom fusion | bytes 2097664 | tf_op jit(solution)/shard_map/scatter | solution.py:124
  62.3 58.9 %all_to_all.10 = bf16[64,16,1024]{2,1,0:T(8,128)(2,1)S(1)} all-to-all(bf16[64,16,1024]{2,1,0:T(8,128)(2,1)} %bitcast.48), channel_id=1, replica_groups=mesh['tile'=64,'rep'=4] {'tile'}, dimensions={0} | all-to-all | bytes 4194304 | tf_op jit(solution)/shard_map/all_to_all | solution.py:127
  121.3 0.0 copy-start.3
  121.3 1.4 copy-done.3
  122.6 0.0 copy-done
  122.6 5.2 %fusion.9 = f32[1024,1408]{1,0:T(8,128)} fusion(bf16[1024,1024]{1,0:T(8,128)(2,1)S(1)} %bitcast.50, bf16[1,1024,1408]{2,1,0:T(8,128)(2,1)S(1)} %copy-done), kind=kOutput, calls=%fused_computation.15 | convolution fusion | flops 2952790016 | bytes 10747904 | tf_op jit(solution)/shard_map/dot_general | solution.py:63
  127.9 13.0 %fusion.13 = bf16[1024,1024]{1,0:T(8,128)(2,1)} fusion(bf16[1,1408,1024]{2,1,0:T(8,128)(2,1)} %param.21, f32[1024,1408]{1,0:T(8,128)} %fusion.9, bf16[1024,1024]{1,0:T(8,128)(2,1)} %bitcast.51, bf16[1,1024,1408]{2,1,0:T(8,128)(2,1)} %param.20), kind=kOutput, calls=%fused_computation.19 | convolution fusion | flops 5915279360 | bytes 15728640 | tf_op jit(solution)/shard_map/dot_general | solution.py:66
  140.8 0.0 copy-start.9
  140.8 8.4 %all-to-all-start.1 = ((bf16[64,16,1024]{2,1,0:T(8,128)(2,1)}), bf16[64,16,1024]{2,1,0:T(8,128)(2,1)}, u32[]{:S(2)}, u32[]{:S(2)}) async-start(bf16[64,16,1024]{2,1,0:T(8,128)(2,1)} %bitcast.49), calls=%async_computation.1 | async-start | bytes 4194304 | tf_op jit(solution)/shard_map/all_to_all | solution.py:131
  149.2 0.1 copy.34
  149.4 0.1 reshape.308
  149.5 0.0 copy-done.9
  149.5 0.1 copy.30
  149.7 47.1 %all-to-all-done.1 = bf16[64,16,1024]{2,1,0:T(8,128)(2,1)} async-done(((bf16[64,16,1024]{2,1,0:T(8,128)(2,1)}), bf16[64,16,1024]{2,1,0:T(8,128)(2,1)}, u32[]{:S(2)}, u32[]{:S(2)}) %all-to-all-start.1) | async-done | bytes 2097184 | tf_op jit(solution)/shard_map/all_to_all | solution.py:131
  196.8 5.3 %gather_fusion = bf16[512,1024]{1,0:T(8,128)(2,1)} fusion(bf16[1024,1024]{1,0:T(8,128)(2,1)} %bitcast.15, s32[1024]{0:T(1024)S(1)} %pad_clamp_fusion), kind=kCustom, calls=%fused_computation | custom fusion | bytes 2099200 | tf_op jit(solution)/shard_map/gather | solution.py:132
  202.2 3.4 %reshape.324 = f32[256,2,1024]{2,1,0:T(2,128)} reshape(bf16[512,1024]{1,0:T(8,128)(2,1)} %gather_fusion) | data formatting | bytes 3145728 | tf_op jit(solution)/shard_map/convert_element_type | solution.py:133
  205.6 4.3 %multiply_reduce_fusion = f32[256,1024]{1,0:T(8,128)S(1)} fusion(f32[256,2,1024]{2,1,0:T(2,128)} %reshape.324, f32[256,2]{1,0:T(8,128)S(1)} %copy.30), kind=kLoop, calls=%fused_computation.18 | loop fusion | flops 786432 | bytes 3147776 | tf_op jit(solution)/shard_map/reduce_sum | solution.py:133
  209.9 1.0 fusion.23
  (10 shorter events, 0.1 us)
Async XLA Ops:
  0.0 122.6 %copy-start = (bf16[1,1024,1408]{2,1,0:T(8,128)(2,1)S(1)}, bf16[1,1024,1408]{2,1,0:T(8,128)(2,1)}, u32[]{:S(2)}) copy-start(bf16[1,1024,1408]{2,1,0:T(8,128)(2,1)} %param.19) | copy-start | bytes 8650756
  0.0 11.4 %copy-start.4 = (bf16[256,1024]{1,0:T(8,128)(2,1)S(1)}, bf16[256,1024]{1,0:T(8,128)(2,1)}, u32[]{:S(2)}) copy-start(bf16[256,1024]{1,0:T(8,128)(2,1)} %param.12) | copy-start | bytes 1572868
  0.0 12.4 %copy-start.7 = (s32[256,2]{0,1:T(2,128)S(1)}, s32[256,2]{0,1:T(2,128)}, u32[]{:S(2)}) copy-start(s32[256,2]{0,1:T(2,128)} %param.17) | copy-start | bytes 6148
  2.3 1.0 copy-start.1
  4.4 15.9 %collective-permute-start = (bf16[128,2048]{1,0:T(8,128)(2,1)}, bf16[128,2048]{1,0:T(8,128)(2,1)}, u32[]{:S(2)}, u32[]{:S(2)}) collective-permute-start(bf16[128,2048]{1,0:T(8,128)(2,1)} %get-tuple-element.9), channel_id=1, source_target_pairs={{0,4},{4,8},{8,12},{12,16},{16,20},{20,24},{24,28},{28,32},{32,36}... | collective-permute-start | bytes 1572872 | tf_op jit(solution)/shard_map/ppermute | solution.py:23
  8.2 23.5 %collective-permute-start.1 = (bf16[128,2048]{1,0:T(8,128)(2,1)}, bf16[128,2048]{1,0:T(8,128)(2,1)}, u32[]{:S(2)}, u32[]{:S(2)}) collective-permute-start(bf16[128,2048]{1,0:T(8,128)(2,1)} %get-tuple-element.10), channel_id=1, source_target_pairs={{4,0},{8,4},{12,8},{16,12},{20,16},{24,20},{28,24},{32,28},{36,32}... | collective-permute-start | bytes 1572872 | tf_op jit(solution)/shard_map/ppermute | solution.py:24
  34.9 4.7 %copy-start.5 = (bf16[256,1024]{0,1:T(8,128)(2,1)S(1)}, bf16[256,1024]{0,1:T(8,128)(2,1)}, u32[]{:S(2)}) copy-start(bf16[256,1024]{0,1:T(8,128)(2,1)} %copy.28) | copy-start | bytes 1572868
  48.0 4.6 %copy-start.2 = (bf16[1024,1024]{1,0:T(8,128)(2,1)S(1)}, bf16[1024,1024]{1,0:T(8,128)(2,1)}, u32[]{:S(2)}) copy-start(bf16[1024,1024]{1,0:T(8,128)(2,1)} %param.15) | copy-start | bytes 6291460
  48.0 4.6 %copy-start.6 = (bf16[256,1024]{1,0:T(8,128)(2,1)S(1)}, bf16[256,1024]{1,0:T(8,128)(2,1)}, u32[]{:S(2)}) copy-start(bf16[256,1024]{1,0:T(8,128)(2,1)} %param.11) | copy-start | bytes 1572868
  52.6 0.9 copy-start.8
  121.3 1.4 copy-start.3
  140.8 8.7 %copy-start.9 = (f32[256,2]{0,1:T(2,128)S(1)}, f32[256,2]{0,1:T(2,128)}, u32[]{:S(2)}) copy-start(f32[256,2]{0,1:T(2,128)} %param.18) | copy-start | bytes 6148
  140.8 56.0 %all-to-all-start.1 = ((bf16[64,16,1024]{2,1,0:T(8,128)(2,1)}), bf16[64,16,1024]{2,1,0:T(8,128)(2,1)}, u32[]{:S(2)}, u32[]{:S(2)}) async-start(bf16[64,16,1024]{2,1,0:T(8,128)(2,1)} %bitcast.49), calls=%async_computation.1 | async-start | bytes 4194304 | tf_op jit(solution)/shard_map/all_to_all | solution.py:131
where the time goes:
time: 215 us; the launch traced here: 211 us
  waiting for transfers between devices  63.9 us (30%)
  blocking collectives  58.9 us (27%)
  matrix products  32 us (15%)
  local copies, waits for them, and re-layouts  31.2 us (15%)
  starting transfers between devices  14.2 us (7%)
  other arithmetic  10.3 us (5%)
    all_to_all x1, blocking collectives, local(): lax.all_to_all(outgoing, 'tile', split_axis=0, concat_axis=0, tiled=True)  58.9 us
    all_to_all x1, waiting for transfers between devices, local(): lax.all_to_all(produced, 'tile', split_axis=0, concat_axis=0, tiled=True)  47.1 us
    dot_general x1, matrix products, expert_rows(): jnp.dot(hidden, down_mat, preferred_element_type=jnp.float32)  13 us
    ppermute x1, waiting for transfers between devices, with_halo(): after = lax.ppermute(initial, axis, down)  11.5 us
    all_to_all x1, starting transfers between devices, local(): lax.all_to_all(produced, 'tile', split_axis=0, concat_axis=0, tiled=True)  8.41 us
    sub x1, matrix products, local_attention(): weights = jnp.exp(scores - highest)  8.39 us
    gather x1, local copies, waits for them, and re-layouts, local(): picked = returned.reshape(-1, model)[positions]  5.35 us
    ppermute x1, waiting for transfers between devices, with_halo(): before = lax.ppermute(last, axis, up)  5.33 us
  transfers between devices with their start and end apart: 3, of which 3 were waited for; matrix products, arithmetic and copies ran while one was open for 2% of the time, Pallas kernels for 0%

commit v1 on v0

--- a/solution.py
+++ b/solution.py
@@ -1,6 +1,8 @@
 import jax
 import jax.numpy as jnp
 from jax import lax
+from jax.experimental import pallas as pl
+from jax.experimental.pallas import tpu as pltpu
 from jax.sharding import PartitionSpec as P
 
 HEADS = 16
@@ -11,6 +13,10 @@
 R_IL = 2
 R_XL = 2
 R_DP = 2
+ZN = 4
+JN = 16
+CAP = 16
+MESH = pl.DeviceIdType.MESH
 
 
 def with_halo(shard, sides, width):
@@ -59,13 +65,6 @@
     return attended.astype(jnp.bfloat16).reshape(query_count, HEADS * HD)
 
 
-def expert_rows(token_rows, gate_mat, up_mat, down_mat):
-    gate_part = jnp.dot(token_rows, gate_mat, preferred_element_type=jnp.float32)
-    up_part = jnp.dot(token_rows, up_mat, preferred_element_type=jnp.float32)
-    hidden = (jax.nn.silu(gate_part) * up_part).astype(jnp.bfloat16)
-    return jnp.dot(hidden, down_mat, preferred_element_type=jnp.float32).astype(jnp.bfloat16)
-
-
 def slot_ranks(routes, experts, block_rows):
     row_count = routes.shape[0]
     expert_ids = jnp.arange(experts, dtype=jnp.int32)
@@ -74,6 +73,363 @@
     hits = hits.reshape(row_count // block_rows, block_rows, experts)
     earlier = (jnp.cumsum(hits, axis=1) - hits).reshape(row_count, experts)
     return jnp.sum(jnp.where(matches, earlier[:, None, :], 0), axis=-1)
+
+
+def tile_order(z, it):
+    low = jnp.where(z == 0, it, lax.rem(it + 1, ZN))
+    mirrored = jnp.where(z == 3, it, lax.rem(it + 1, ZN))
+    return jnp.where(z < 2, low, 3 - mirrored)
+
+
+def moe_kernel(
+    x_ref,
+    res_ref,
+    meta_ref,
+    wg_hbm,
+    wu_hbm,
+    wd_hbm,
+    out_ref,
+    wg,
+    wu,
+    wd,
+    meta_all,
+    x_all,
+    disp,
+    recv,
+    eout,
+    ret,
+    own,
+    rs_out,
+    rs_in,
+    w_sem,
+    meta_send,
+    meta_recv,
+    ag_send,
+    fw_send,
+    ag_recv,
+    xs,
+    xr,
+    ys,
+    yr,
+    rs_send,
+    rs_recv,
+):
+    t = lax.axis_index("tile")
+    z = lax.rem(t, ZN)
+    j = lax.div(t, ZN)
+    rows = x_ref.shape[0]
+    model = x_ref.shape[1]
+
+    w_copies = [
+        pltpu.make_async_copy(wg_hbm.at[0], wg, w_sem.at[0]),
+        pltpu.make_async_copy(wu_hbm.at[0], wu, w_sem.at[1]),
+        pltpu.make_async_copy(wd_hbm.at[0], wd, w_sem.at[2]),
+    ]
+
+    barrier = pltpu.get_barrier_semaphore()
+
+    def z_peer(d):
+        return j * ZN + lax.rem(z + d, ZN)
+
+    def plane_peer(d):
+        return lax.rem(j + d, JN)
+
+    def greet_plane(d, carry):
+        pl.semaphore_signal(
+            barrier, inc=1, device_id={"tile": plane_peer(d) * ZN + z}, device_id_type=MESH
+        )
+        return carry
+
+    lax.fori_loop(1, JN, greet_plane, 0)
+    for d in range(1, ZN):
+        pl.semaphore_signal(barrier, inc=1, device_id={"tile": z_peer(d)}, device_id_type=MESH)
+    for c in w_copies:
+        c.start()
+    pl.semaphore_wait(barrier, JN - 1 + ZN - 1)
+
+    def send_tile(src, slot, to, send_sem):
+        return pltpu.make_async_remote_copy(
+            src_ref=src,
+            dst_ref=x_all.at[slot],
+            send_sem=send_sem,
+            recv_sem=ag_recv.at[slot],
+            device_id={"tile": to},
+            device_id_type=MESH,
+        )
+
+    def send_meta(d):
+        return pltpu.make_async_remote_copy(
+            src_ref=meta_ref,
+            dst_ref=meta_all.at[z],
+            send_sem=meta_send.at[d - 1],
+            recv_sem=meta_recv.at[z],
+            device_id={"tile": z_peer(d)},
+            device_id_type=MESH,
+        )
+
+    for d in range(1, ZN):
+        send_meta(d).start()
+
+    @pl.when(z < ZN - 1)
+    def _():
+        send_tile(x_ref, z, t + 1, ag_send.at[0]).start()
+
+    @pl.when(z > 0)
+    def _():
+        send_tile(x_ref, z, t - 1, ag_send.at[1]).start()
+
+    meta_all[z] = meta_ref[...]
+    x_all[z] = x_ref[...]
+
+    def tile_arrived(slot):
+        send_tile(x_ref, slot, t, ag_send.at[0]).wait_recv()
+
+    def arrive(distance):
+        @pl.when(z - distance >= 0)
+        def _():
+            tile_arrived(z - distance)
+
+            @pl.when(z + 1 < ZN)
+            def _():
+                send_tile(x_all.at[z - distance], z - distance, t + 1, fw_send.at[z - distance]).start()
+
+        @pl.when(z + distance < ZN)
+        def _():
+            tile_arrived(z + distance)
+
+            @pl.when(z - 1 >= 0)
+            def _():
+                send_tile(x_all.at[z + distance], z + distance, t - 1, fw_send.at[z + distance]).start()
+
+    def dispatch_copy(it, d):
+        return pltpu.make_async_remote_copy(
+            src_ref=disp.at[it, plane_peer(d)],
+            dst_ref=recv.at[it, j],
+            send_sem=xs.at[it],
+            recv_sem=xr.at[it],
+            device_id={"tile": plane_peer(d) * ZN + z},
+            device_id_type=MESH,
+        )
+
+    def return_copy(it, d):
+        return pltpu.make_async_remote_copy(
+            src_ref=eout.at[it, plane_peer(d)],
+            dst_ref=ret.at[it, j],
+            send_sem=ys.at[it],
+            recv_sem=yr.at[it],
+            device_id={"tile": plane_peer(d) * ZN + z},
+            device_id_type=MESH,
+        )
+
+    def all_of(src, dst, it, send_sem, recv_sem):
+        return pltpu.make_async_remote_copy(
+            src_ref=src.at[it, pl.ds(0, JN - 1)],
+            dst_ref=dst.at[it, pl.ds(0, JN - 1)],
+            send_sem=send_sem.at[it],
+            recv_sem=recv_sem.at[it],
+            device_id={"tile": t},
+            device_id_type=MESH,
+        )
+
+    slots = JN * CAP
+    slot_of = lax.broadcasted_iota(jnp.int32, (slots, rows), 0).astype(jnp.float32)
+
+    def stage_dispatch(it):
+        for distance in range(1, ZN):
+
+            @pl.when(it == distance)
+            def _():
+                arrive(distance)
+
+        s = tile_order(z, it)
+        base = (z * slots).astype(jnp.float32)
+        meta = meta_all[s] - base
+        picks = (slot_of == meta[0:1]) | (slot_of == meta[1:2])
+        table = picks.astype(jnp.float32).astype(jnp.bfloat16)
+        picked = jnp.dot(table, x_all[s], preferred_element_type=jnp.float32).astype(jnp.bfloat16)
+        disp[it] = picked.reshape(JN, CAP, model)
+
+        def start(d, carry):
+            dispatch_copy(it, d).start()
+            return carry
+
+        lax.fori_loop(1, JN, start, 0)
+        recv[it, j] = disp[it, j]
+
+    def stage_expert(it):
+        all_of(disp, recv, it, xs, xr).wait_recv()
+        zrows = recv[it].reshape(slots, model)
+        gate_part = jnp.dot(zrows, wg[...], preferred_element_type=jnp.float32)
+        up_part = jnp.dot(zrows, wu[...], preferred_element_type=jnp.float32)
+        hidden = (gate_part / (1.0 + jnp.exp(-gate_part)) * up_part).astype(jnp.bfloat16)
+        result = jnp.dot(hidden, wd[...], preferred_element_type=jnp.float32)
+        eout[it] = result.astype(jnp.bfloat16).reshape(JN, CAP, model)
+
+        def start(d, carry):
+            return_copy(it, d).start()
+            return carry
+
+        lax.fori_loop(1, JN, start, 0)
+        ret[it, j] = eout[it, j]
+
+    def rs_copy(it):
+        s = tile_order(z, it)
+        return pltpu.make_async_remote_copy(
+            src_ref=rs_out.at[it],
+            dst_ref=rs_in.at[z],
+            send_sem=rs_send.at[it],
+            recv_sem=rs_recv.at[z],
+            device_id={"tile": j * ZN + s},
+            device_id_type=MESH,
+        )
+
+    def stage_combine(it):
+        all_of(eout, ret, it, ys, yr).wait_recv()
+        s = tile_order(z, it)
+        base = (z * slots).astype(jnp.float32)
+        meta = meta_all[s]
+        pos = meta[0:2] - base
+        weights = jnp.where(slot_of == pos[0:1], meta[2:3], 0.0) + jnp.where(
+            slot_of == pos[1:2], meta[3:4], 0.0
+        )
+        part = lax.dot_general(
+            weights.astype(jnp.bfloat16),
+            ret[it].reshape(slots, model),
+            (((0,), (0,)), ((), ())),
+            preferred_element_type=jnp.float32,
+        )
+
+        @pl.when(it == 0)
+        def _():
+            own[...] = part
+
+        @pl.when(it > 0)
+        def _():
+            rs_out[it] = part.astype(jnp.bfloat16)
+            rs_copy(it).start()
+
+    def step(it, carry):
+        @pl.when(it == 0)
+        def _():
+            for d in range(1, ZN):
+                src = lax.rem(z + d, ZN)
+                pltpu.make_async_remote_copy(
+                    src_ref=meta_ref,
+                    dst_ref=meta_all.at[src],
+                    send_sem=meta_send.at[0],
+                    recv_sem=meta_recv.at[src],
+                    device_id={"tile": t},
+                    device_id_type=MESH,
+                ).wait_recv()
+            for c in w_copies:
+                c.wait()
+
+        @pl.when(it < ZN)
+        def _():
+            stage_dispatch(it)
+
+        @pl.when(it > 0)
+        def _():
+            stage_combine(it - 1)
+
+        @pl.when(it < ZN)
+        def _():
+            stage_expert(it)
+
+        return carry
+
+    lax.fori_loop(0, ZN + 1, step, 0)
+
+    total = own[...] + res_ref[...].astype(jnp.float32)
+    for d in range(1, ZN):
+        src = lax.rem(z + d, ZN)
+        pltpu.make_async_remote_copy(
+            src_ref=rs_out.at[0],
+            dst_ref=rs_in.at[src],
+            send_sem=rs_send.at[0],
+            recv_sem=rs_recv.at[src],
+            device_id={"tile": t},
+            device_id_type=MESH,
+        ).wait_recv()
+        total = total + rs_in[src].astype(jnp.float32)
+    out_ref[...] = total.astype(jnp.bfloat16)
+
+    for d in range(1, ZN):
+        send_meta(d).wait_send()
+
+    @pl.when(z < ZN - 1)
+    def _():
+        send_tile(x_ref, z, t + 1, ag_send.at[0]).wait_send()
+
+    @pl.when(z > 0)
+    def _():
+        send_tile(x_ref, z, t - 1, ag_send.at[1]).wait_send()
+
+    for distance in range(1, ZN):
+
+        @pl.when((z - distance >= 0) & (z + 1 < ZN))
+        def _():
+            send_tile(x_all.at[z - distance], z - distance, t, fw_send.at[z - distance]).wait_send()
+
+        @pl.when((z + distance < ZN) & (z - 1 >= 0))
+        def _():
+            send_tile(x_all.at[z + distance], z + distance, t, fw_send.at[z + distance]).wait_send()
+
+    def drain(it, carry):
+        all_of(disp, recv, it, xs, xr).wait_send()
+        all_of(eout, ret, it, ys, yr).wait_send()
+
+        @pl.when(it > 0)
+        def _():
+            rs_copy(it).wait_send()
+
+        return carry
+
+    lax.fori_loop(0, ZN, drain, 0)
+
+
+def routed_experts(normed, residual, meta, w_gate, w_up, w_down):
+    rows, model = normed.shape
+    wide = w_gate.shape[2]
+    bf16 = jnp.bfloat16
+    vmem = pl.BlockSpec(memory_space=pltpu.VMEM)
+    anywhere = pl.BlockSpec(memory_space=pl.ANY)
+    dma = pltpu.SemaphoreType.DMA
+    return pl.pallas_call(
+        moe_kernel,
+        out_shape=jax.ShapeDtypeStruct((rows, model), bf16),
+        in_specs=[vmem, vmem, vmem, anywhere, anywhere, anywhere],
+        out_specs=vmem,
+        scratch_shapes=[
+            pltpu.VMEM((model, wide), bf16),
+            pltpu.VMEM((model, wide), bf16),
+            pltpu.VMEM((wide, model), bf16),
+            pltpu.VMEM((ZN, 8, rows), jnp.float32),
+            pltpu.VMEM((ZN, rows, model), bf16),
+            pltpu.VMEM((ZN, JN, CAP, model), bf16),
+            pltpu.VMEM((ZN, JN, CAP, model), bf16),
+            pltpu.VMEM((ZN, JN, CAP, model), bf16),
+            pltpu.VMEM((ZN, JN, CAP, model), bf16),
+            pltpu.VMEM((rows, model), jnp.float32),
+            pltpu.VMEM((ZN, rows, model), bf16),
+            pltpu.VMEM((ZN, rows, model), bf16),
+            dma((3,)),
+            dma((3,)),
+            dma((ZN,)),
+            dma((2,)),
+            dma((ZN,)),
+            dma((ZN,)),
+            dma((ZN,)),
+            dma((ZN,)),
+            dma((ZN,)),
+            dma((ZN,)),
+            dma((ZN,)),
+            dma((ZN,)),
+        ],
+        compiler_params=pltpu.CompilerParams(
+            collective_id=1, has_side_effects=True, vmem_limit_bytes=56 * 1024 * 1024
+        ),
+    )(normed, residual, meta, w_gate, w_up, w_down)
 
 
 def local(
@@ -108,30 +464,14 @@
     normed = (resid_float * lax.rsqrt(mean_square + 1e-06) * norm_gain[None, :]).astype(
         jnp.bfloat16
     )
-    route_width = routes.shape[1]
     block_rows = row_count // 2
-    capacity = row_count * route_width // tiles
     slot_rank = slot_ranks(routes, tiles, block_rows)
-    gate_mat = w_gate[0]
-    up_mat = w_up[0]
-    down_mat = w_down[0]
     half_index = (jnp.arange(row_count, dtype=jnp.int32) // block_rows)[:, None]
-    positions = routes * (2 * capacity) + half_index * capacity + slot_rank
-    copies = jnp.broadcast_to(normed[:, None, :], (row_count, route_width, model)).reshape(
-        -1, model
-    )
-    outgoing = (
-        jnp.zeros((tiles * 2 * capacity, model), jnp.bfloat16).at[positions.reshape(-1)].set(copies)
-    )
-    outgoing = outgoing.reshape(tiles, 2 * capacity, model)
-    received = lax.all_to_all(outgoing, "tile", split_axis=0, concat_axis=0, tiled=True)
-    produced = expert_rows(received.reshape(-1, model), gate_mat, up_mat, down_mat).reshape(
-        received.shape
-    )
-    returned = lax.all_to_all(produced, "tile", split_axis=0, concat_axis=0, tiled=True)
-    picked = returned.reshape(-1, model)[positions]
-    combined = jnp.sum(route_gates[:, :, None] * picked.astype(jnp.float32), axis=1)
-    return (resid_float + combined).astype(jnp.bfloat16)
+    pos = (
+        routes % ZN * (JN * CAP) + routes // ZN * CAP + half_index * (CAP // 2) + slot_rank
+    ).astype(jnp.float32)
+    meta = jnp.concatenate([pos.T, route_gates.T, jnp.zeros((4, row_count), jnp.float32)], axis=0)
+    return routed_experts(normed, residual, meta, w_gate, w_up, w_down)
 
 
 def solution(mesh):

time: 215 us -> 165 us (0.77); the launches traced: 211 us -> 164 us
  Pallas kernels: 0 us -> 121 us
  blocking collectives: 58.9 us -> 0 us
  waiting for transfers between devices: 63.9 us -> 8.12 us
  matrix products: 32 us -> 13.1 us
  local copies, waits for them, and re-layouts: 31.2 us -> 12.4 us
  starting transfers between devices: 14.2 us -> 5.83 us
  other arithmetic: 10.3 us -> 3.79 us
    pallas_call x0 -> x1, Pallas kernels: none -> 121 us  [routed_experts(): pl.pallas_call(moe_kernel, out_shape=jax.ShapeDtypeStruct((rows, model),...]
    all_to_all x1 -> x0, blocking collectives: 58.9 us -> none  [local(): lax.all_to_all(outgoing, 'tile', split_axis=0, concat_axis=0, tiled=True)]
    all_to_all x1 -> x0, waiting for transfers between devices: 47.1 us -> none  [local(): lax.all_to_all(produced, 'tile', split_axis=0, concat_axis=0, tiled=True)]
    dot_general x2 -> x0, matrix products: 18.2 us -> none  [the longest x1 13 us: expert_rows(): jnp.dot(hidden, down_mat, preferred_element_type=jnp.float32)]
    all_to_all x1 -> x0, starting transfers between devices: 8.41 us -> none  [local(): lax.all_to_all(produced, 'tile', split_axis=0, concat_axis=0, tiled=True)]
    gather x1 -> x0, local copies, waits for them, and re-layouts: 5.35 us -> none  [local(): picked = returned.reshape(-1, model)[positions]]
    scatter x1 -> x0, local copies, waits for them, and re-layouts: 4.82 us -> none  [local(): jnp.zeros((tiles * 2 * capacity, model), jnp.bfloat16)]
    ppermute x1, waiting for transfers between devices: 5.33 us -> 0.8 us  [with_halo(): before = lax.ppermute(last, axis, up)]
  transfers between devices with their start and end apart: 3 -> 2, of which waited for: 3 -> 2; matrix products, arithmetic and copies ran while one was open for 2% -> 2% of each run, Pallas kernels for 0% -> 0%
where the time goes in v1:
time: 165 us; the launch traced here: 164 us
  Pallas kernels  121 us (73%)
  matrix products  13.1 us (8%)
  local copies, waits for them, and re-layouts  12.4 us (8%)
  waiting for transfers between devices  8.12 us (5%)
  starting transfers between devices  5.83 us (4%)
  other arithmetic  3.79 us (2%)
    pallas_call x1, Pallas kernels, routed_experts(): pl.pallas_call(moe_kernel, out_shape=jax.ShapeDtypeStruct((rows, model),...  121 us
    sub x1, matrix products, local_attention(): weights = jnp.exp(scores - highest)  8 us
    ppermute x1, waiting for transfers between devices, with_halo(): after = lax.ppermute(initial, axis, down)  7.32 us
    unnamed x17, local copies, waits for them, and re-layouts  5.2 us
    dot_general x1, matrix products, local_attention(): jnp.einsum('hqk,khd->qhd', probs, value_heads, preferred_element_type=jnp...  4.29 us
    ppermute x1, starting transfers between devices, with_halo(): before = lax.ppermute(last, axis, up)  3.83 us
  transfers between devices with their start and end apart: 2, of which 2 were waited for; matrix products, arithmetic and copies ran while one was open for 2% of the time, Pallas kernels for 0%

profile of v1, /device:TPU:64, one launch (start us, length us, event | category | flops | bytes accessed | tf_op | source)
XLA Modules:
  0.0 164.2 jit_solution(2265793929688038147)
XLA Ops:
  0.0 0.0 copy-start
  0.0 0.0 copy-start.4
  0.0 0.0 copy-start.6
  0.0 1.2 constant_dynamic-update-slice_fusion.1
  1.2 1.1 constant_dynamic-update-slice_fusion
  2.3 1.0 fusion.33
  3.4 2.0 %collective-permute-start.1 = (bf16[128,2048]{1,0:T(8,128)(2,1)}, bf16[128,2048]{1,0:T(8,128)(2,1)}, u32[]{:S(2)}, u32[]{:S(2)}) collective-permute-start(bf16[128,2048]{1,0:T(8,128)(2,1)} %get-tuple-element.8), channel_id=1, source_target_pairs={{4,0},{8,4},{12,8},{16,12},{20,16},{24,20},{28,24},{32,28},{36,32}... | collective-permute-start | bytes 1572872 | tf_op jit(solution)/shard_map/ppermute | solution.py:30
  5.4 3.8 %collective-permute-start = (bf16[128,2048]{1,0:T(8,128)(2,1)}, bf16[128,2048]{1,0:T(8,128)(2,1)}, u32[]{:S(2)}, u32[]{:S(2)}) collective-permute-start(bf16[128,2048]{1,0:T(8,128)(2,1)} %get-tuple-element.7), channel_id=1, source_target_pairs={{0,4},{4,8},{8,12},{12,16},{16,20},{20,24},{24,28},{28,32},{32,36}... | collective-permute-start | bytes 1572872 | tf_op jit(solution)/shard_map/ppermute | solution.py:29
  9.3 2.1 %copy.24 = bf16[256,1024]{0,1:T(8,128)(2,1)} copy(bf16[256,1024]{1,0:T(8,128)(2,1)} %param.12) | data formatting | bytes 1048576 | tf_op args[1]
  11.3 0.0 copy-done.4
  11.4 0.1 copy.29
  11.5 0.2 reduce_window_sum.13
  11.7 0.1 copy.27
  11.8 0.1 pad.2.clone
  11.9 0.0 copy-done.6
  11.9 0.7 maximum_maximum_fusion.meta_ref
  12.6 0.4 fusion.15
  13.0 7.3 %collective-permute-done.1 = bf16[128,2048]{1,0:T(8,128)(2,1)} collective-permute-done((bf16[128,2048]{1,0:T(8,128)(2,1)}, bf16[128,2048]{1,0:T(8,128)(2,1)}, u32[]{:S(2)}, u32[]{:S(2)}) %collective-permute-start.1) | collective-permute-done | bytes 524320 | tf_op jit(solution)/shard_map/ppermute | solution.py:30
  20.4 0.8 collective-permute-done
  21.2 1.4 pad_maximum_fusion
  22.6 1.2 fusion.32
  23.8 2.4 %copy.22 = bf16[512,1024]{0,1:T(8,128)(2,1)} copy(bf16[512,1024]{1,0:T(8,128)(2,1)} %get-tuple-element.6) | data formatting | bytes 2097152 | tf_op jit(solution)/shard_map/slice | solution.py:456
  26.1 1.3 copy.23
  27.4 0.0 copy-start.2
  27.4 8.0 %fusion.34 = (f32[16,256]{1,0:T(8,128)S(1)}, f32[16,256,512]{1,2,0:T(8,128)}) fusion(pred[256,512]{0,1:T(8,128)(4,1)S(1)} %fusion.15, bf16[512,16,64]{0,2,1:T(8,128)(2,1)} %bitcast.30, bf16[256,16,64]{0,2,1:T(8,128)(2,1)} %bitcast.31), kind=kOutput, calls=%fused_computation.82 | convolution fusion | flops 278921728 | bytes 10108928 | tf_op jit(solution)/shard_map/sub | solution.py:60
  35.4 0.0 copy-done.2
  35.4 0.0 copy-start.3
  35.4 0.0 copy-start.5
  35.4 4.3 %fusion.6 = bf16[16,64,256]{2,1,0:T(8,128)(2,1)S(1)} fusion(bf16[512,16,64]{0,2,1:T(8,128)(2,1)S(1)} %bitcast.29, f32[16,256,512]{1,2,0:T(8,128)} %get-tuple-element.10, f32[16,256]{1,0:T(8,128)S(1)} %get-tuple-element.9), kind=kOutput, calls=%fused_computation.13 | convolution fusion | flops 272891904 | bytes 9977856 | tf_op jit(solution)/shard_map/hqk,khd->qhd/dot_general | solution.py:64
  39.7 0.0 copy-done
  39.7 0.0 copy-done.3
  39.7 0.8 fusion.8
  40.6 0.0 copy-start.1
  40.6 0.0 copy-done.5
  40.6 1.0 fusion.10.x_ref
  41.6 0.0 copy-done.1
  41.6 120.7 %shard_map.109 = bf16[256,1024]{1,0:T(8,128)(2,1)} custom-call(bf16[256,1024]{1,0:T(8,128)(2,1)} %fusion.10.x_ref, bf16[256,1024]{1,0:T(8,128)(2,1)} %copy-done.1, f32[8,256]{1,0:T(8,128)} %maximum_maximum_fusion.meta_ref, bf16[1,1024,1408]{2,1,0:T(8,128)(2,1)} %wg_hbm.1, bf16[1,1024,1408]{2,1,0:T(8,128)(2,1)} %wu_hbm.1, bf16[1,1408,1024]{2,1,0:T(8,128)(2,1)} %wd_hbm.1), custom_call_target="tpu_custom_call" | custom-call | tf_op jit(solution)/shard_map/pallas_call | solution.py:398
  162.3 1.9 %copy.32 = bf16[256,1024]{1,0:T(8,128)(2,1)} copy(bf16[256,1024]{1,0:T(8,128)(2,1)} %shard_map.109) | data formatting | bytes 1048576
  (12 shorter events, 0.1 us)
Async XLA Ops:
  0.0 39.7 %copy-start = (bf16[1024,1024]{1,0:T(8,128)(2,1)S(1)}, bf16[1024,1024]{1,0:T(8,128)(2,1)}, u32[]{:S(2)}) copy-start(bf16[1024,1024]{1,0:T(8,128)(2,1)} %param.15) | copy-start | bytes 6291460
  0.0 11.3 %copy-start.4 = (s32[256,2]{0,1:T(2,128)S(1)}, s32[256,2]{0,1:T(2,128)}, u32[]{:S(2)}) copy-start(s32[256,2]{0,1:T(2,128)} %param.17) | copy-start | bytes 6148
  0.0 11.9 %copy-start.6 = (f32[256,2]{0,1:T(2,128)S(1)}, f32[256,2]{0,1:T(2,128)}, u32[]{:S(2)}) copy-start(f32[256,2]{0,1:T(2,128)} %param.18) | copy-start | bytes 6148
  3.4 17.0 %collective-permute-start.1 = (bf16[128,2048]{1,0:T(8,128)(2,1)}, bf16[128,2048]{1,0:T(8,128)(2,1)}, u32[]{:S(2)}, u32[]{:S(2)}) collective-permute-start(bf16[128,2048]{1,0:T(8,128)(2,1)} %get-tuple-element.8), channel_id=1, source_target_pairs={{4,0},{8,4},{12,8},{16,12},{20,16},{24,20},{28,24},{32,28},{36,32}... | collective-permute-start | bytes 1572872 | tf_op jit(solution)/shard_map/ppermute | solution.py:30
  5.4 15.8 %collective-permute-start = (bf16[128,2048]{1,0:T(8,128)(2,1)}, bf16[128,2048]{1,0:T(8,128)(2,1)}, u32[]{:S(2)}, u32[]{:S(2)}) collective-permute-start(bf16[128,2048]{1,0:T(8,128)(2,1)} %get-tuple-element.7), channel_id=1, source_target_pairs={{0,4},{4,8},{8,12},{12,16},{16,20},{20,24},{24,28},{28,32},{32,36}... | collective-permute-start | bytes 1572872 | tf_op jit(solution)/shard_map/ppermute | solution.py:29
  27.4 8.0 %copy-start.2 = (bf16[512,1024]{0,1:T(8,128)(2,1)S(1)}, bf16[512,1024]{0,1:T(8,128)(2,1)}, u32[]{:S(2)}) copy-start(bf16[512,1024]{0,1:T(8,128)(2,1)} %copy.22) | copy-start | bytes 3145732
  35.4 4.3 %copy-start.3 = (bf16[256,1024]{1,0:T(8,128)(2,1)S(1)}, bf16[256,1024]{1,0:T(8,128)(2,1)}, u32[]{:S(2)}) copy-start(bf16[256,1024]{1,0:T(8,128)(2,1)} %param.11) | copy-start | bytes 1572868
  35.4 5.2 %copy-start.5 = (f32[1024]{0:T(1024)S(1)}, f32[1024]{0:T(1024)}, u32[]{:S(2)}) copy-start(f32[1024]{0:T(1024)} %param.16) | copy-start | bytes 12292
  40.6 1.0 copy-start.1

commit v2 on v1

v2 whole, which is shorter than its diff:
```python
import jax
import jax.numpy as jnp
from jax import lax
from jax.experimental import pallas as pl
from jax.experimental.pallas import tpu as pltpu
from jax.sharding import PartitionSpec as P

HEADS = 16
HD = 64
IL_DEV = 4
XL = 8
DP = 8
R_IL = 2
R_XL = 2
R_DP = 2
ZN = 4
JN = 16
CAP = 16
MESH = pl.DeviceIdType.MESH


def tile_order(z, it):
    low = jnp.where(z == 0, it, lax.rem(it + 1, ZN))
    mirrored = jnp.where(z == 3, it, lax.rem(it + 1, ZN))
    return jnp.where(z < 2, low, 3 - mirrored)


def layer_kernel(
    x_hbm,
    q_hbm,
    k_hbm,
    v_hbm,
    ow_hbm,
    gain_ref,
    routes_ref,
    gates_ref,
    wg_hbm,
    wu_hbm,
    wd_hbm,
    out_ref,
    x_in,
    q_in,
    ke,
    ve,
    ow,
    att,
    near,
    wg,
    wu,
    wd,
    meta_own,
    meta_all,
    x_all,
    resid,
    disp,
    recv,
    eout,
    ret,
    own,
    rs_out,
    rs_in,
    l_sem,
    h_send,
    h_recv,
    meta_send,
    meta_recv,
    ag_send,
    fw_send,
    ag_recv,
    xs,
    xr,
    ys,
    yr,
    rs_send,
    rs_recv,
):
    t = lax.axis_index("tile")
    tiles = lax.axis_size("tile")
    z = lax.rem(t, ZN)
    j = lax.div(t, ZN)
    rows = x_in.shape[0]
    model = x_in.shape[1]
    plane = XL * DP
    halo = R_IL * plane
    keys = (2 * R_IL + 1) * plane
    bf16 = jnp.bfloat16
    f32 = jnp.float32

    def local_copy(src, dst, n):
        return pltpu.make_async_copy(src, dst, l_sem.at[n])

    early = [
        local_copy(k_hbm, ke.at[pl.ds(halo, rows)], 0),
        local_copy(v_hbm, ve.at[pl.ds(halo, rows)], 1),
        local_copy(q_hbm, q_in, 2),
    ]
    mid = [local_copy(x_hbm, x_in, 3), local_copy(ow_hbm, ow, 4)]
    late = [
        local_copy(wg_hbm.at[0], wg, 5),
        local_copy(wu_hbm.at[0], wu, 6),
        local_copy(wd_hbm.at[0], wd, 7),
    ]

    barrier = pltpu.get_barrier_semaphore()

    def greet(tile):
        pl.semaphore_signal(barrier, inc=1, device_id={"tile": tile}, device_id_type=MESH)

    def z_peer(d):
        return j * ZN + lax.rem(z + d, ZN)

    def plane_peer(d):
        return lax.rem(j + d, JN)

    @pl.when(t > 0)
    def _():
        greet(t - 1)

    @pl.when(t < tiles - 1)
    def _():
        greet(t + 1)

    for d in range(1, ZN):
        greet(z_peer(d))

    def greet_plane(d, carry):
        greet(plane_peer(d) * ZN + z)
        return carry

    lax.fori_loop(1, JN, greet_plane, 0)
    for c in early + mid + late:
        c.start()
    pl.semaphore_wait(
        barrier,
        JN - 1 + ZN - 1 + jnp.where(t > 0, 1, 0) + jnp.where(t < tiles - 1, 1, 0),
    )

    pieces = (
        (rows - plane, halo - plane),
        (rows - 2 * plane, halo - 2 * plane),
        (0, halo + rows),
        (plane, halo + rows + plane),
    )

    def halo_copy(n, kv):
        src, dst = pieces[n]
        return pltpu.make_async_remote_copy(
            src_ref=(k_hbm, v_hbm)[kv].at[pl.ds(src, plane)],
            dst_ref=(ke, ve)[kv].at[pl.ds(dst, plane)],
            send_sem=h_send.at[2 * n + kv],
            recv_sem=h_recv.at[2 * n + kv],
            device_id={"tile": t + 1 if n < 2 else t - 1},
            device_id_type=MESH,
        )

    for far in range(2):
        for kv in range(2):

            @pl.when(t < tiles - 1)
            def _():
                halo_copy(far, kv).start()

            @pl.when(t > 0)
            def _():
                halo_copy(2 + far, kv).start()

    @pl.when(t == 0)
    def _():
        ke[0:halo] = jnp.zeros((halo, model), bf16)
        ve[0:halo] = jnp.zeros((halo, model), bf16)

    @pl.when(t == tiles - 1)
    def _():
        ke[halo + rows :] = jnp.zeros((halo, model), bf16)
        ve[halo + rows :] = jnp.zeros((halo, model), bf16)

    def halo_wait(n):
        present = t > 0 if n < 2 else t < tiles - 1

        @pl.when(present)
        def _():
            for kv in range(2):
                halo_copy(n, kv).wait_recv()

    block = rows // 2
    ti = lax.broadcasted_iota(jnp.int32, (rows, rows), 0)
    tj = lax.broadcasted_iota(jnp.int32, (rows, rows), 1)
    same = ti == tj
    before = (ti < tj) & ((ti < block) == (tj < block))
    route = routes_ref[...].astype(f32)
    cols = [
        jnp.sum(jnp.where(same, route[k : k + 1], 0.0), axis=1, keepdims=True) for k in range(2)
    ]
    half = jnp.where(lax.broadcasted_iota(jnp.int32, (1, rows), 1) < block, 0.0, CAP // 2)
    for k in range(2):
        r = route[k : k + 1]
        hits = jnp.where(cols[0] == r, 1.0, 0.0) + jnp.where(cols[1] == r, 1.0, 0.0)
        rank = jnp.sum(jnp.where(before, hits, 0.0), axis=0, keepdims=True)
        column = jnp.floor(r * (1.0 / ZN))
        meta_own[k : k + 1, :] = (r - ZN * column) * (JN * CAP) + column * CAP + half + rank
    meta_own[2:4, :] = gates_ref[...]
    meta_own[4:8, :] = jnp.zeros((4, rows), f32)

    def send_meta(d):
        return pltpu.make_async_remote_copy(
            src_ref=meta_own,
            dst_ref=meta_all.at[z],
            send_sem=meta_send.at[d - 1],
            recv_sem=meta_recv.at[z],
            device_id={"tile": z_peer(d)},
            device_id_type=MESH,
        )

    for d in range(1, ZN):
        send_meta(d).start()
    meta_all[z] = meta_own[...]

    qi = lax.rem(lax.broadcasted_iota(jnp.int32, (4 * plane, keys), 0), plane)
    ki = lax.broadcasted_iota(jnp.int32, (4 * plane, keys), 1)
    kp = lax.rem(ki, plane)
    close = (jnp.abs(lax.div(qi, DP) - lax.div(kp, DP)) <= R_XL) & (
        jnp.abs(lax.rem(qi, DP) - lax.rem(kp, DP)) <= R_DP
    )
    near[...] = jnp.where(close, 0.0, -1e30)
    kcol = lax.div(lax.broadcasted_iota(jnp.int32, (1, keys), 1), plane)
    lane_head = lax.div(lax.broadcasted_iota(jnp.int32, (plane, 4 * HD), 1), HD)

    def attend(i):
        outside = ((t == 0) & (kcol < R_IL - i)) | (
            (t == tiles - 1) & (kcol > IL_DEV - 1 + R_IL - i)
        )
        bias = near[...] + jnp.where(outside, -1e30, 0.0)
        for g in range(HEADS // 4):
            lanes = slice(g * 4 * HD, (g + 1) * 4 * HD)
            q4 = q_in[i * plane : (i + 1) * plane, lanes].astype(f32) * (1.0 / HD**0.5)
            stacked = jnp.concatenate(
                [jnp.where(lane_head == h, q4, 0.0).astype(bf16) for h in range(4)], axis=0
            )
            window = slice(i * plane, i * plane + keys)
            scores = lax.dot_general(
                stacked,
                ke[window, lanes],
                (((1,), (1,)), ((), ())),
                preferred_element_type=f32,
            )
            scores = scores + bias
            highest = jnp.max(scores, axis=1, keepdims=True)
            weights = jnp.exp(scores - highest)
            totals = jnp.sum(weights, axis=1, keepdims=True)
            probs = (weights * (1.0 / totals)).astype(bf16)
            mixed = jnp.dot(probs, ve[window, lanes], preferred_element_type=f32)
            picked = mixed[0:plane]
            for h in range(1, 4):
                picked = jnp.where(lane_head == h, mixed[h * plane : (h + 1) * plane], picked)
            att[i * plane : (i + 1) * plane, lanes] = picked.astype(bf16)

    def finish(parts):
        take = lambda ref: jnp.concatenate([ref[lo : lo + n] for lo, n in parts], axis=0)
        sums = take(x_in).astype(f32) + jnp.dot(take(att), ow[...], preferred_element_type=f32)
        rounded = sums.astype(bf16)
        wide = rounded.astype(f32)
        mean_square = jnp.mean(wide * wide, axis=1, keepdims=True)
        normed = (wide * lax.rsqrt(mean_square + 1e-06) * gain_ref[...]).astype(bf16)
        at = 0
        for lo, n in parts:
            resid[lo : lo + n] = rounded[at : at + n]
            x_all[z, lo : lo + n] = normed[at : at + n]
            at += n

    chunks = ((plane, 2 * plane), (0, plane), (3 * plane, plane))

    def tile_copy(slot, c, to, send_sem):
        lo, n = chunks[c]
        return pltpu.make_async_remote_copy(
            src_ref=x_all.at[slot, pl.ds(lo, n)],
            dst_ref=x_all.at[slot, pl.ds(lo, n)],
            send_sem=send_sem,
            recv_sem=ag_recv.at[slot, c],
            device_id={"tile": to},
            device_id_type=MESH,
        )

    def send_own(c):
        @pl.when(z < ZN - 1)
        def _():
            tile_copy(z, c, t + 1, ag_send.at[0, c]).start()

        @pl.when(z > 0)
        def _():
            tile_copy(z, c, t - 1, ag_send.at[1, c]).start()

    for c in early:
        c.wait()
    halo_wait(0)
    attend(1)
    halo_wait(2)
    attend(2)
    for c in mid:
        c.wait()
    finish([chunks[0]])
    send_own(0)
    halo_wait(1)
    attend(0)
    halo_wait(3)
    attend(3)
    finish([chunks[1], chunks[2]])
    send_own(1)
    send_own(2)

    def arrive(distance):
        for c in range(len(chunks)):

            @pl.when(z - distance >= 0)
            def _():
                tile_copy(z - distance, c, t, ag_send.at[0, c]).wait_recv()

                @pl.when(z + 1 < ZN)
                def _():
                    tile_copy(z - distance, c, t + 1, fw_send.at[z - distance, c]).start()

            @pl.when(z + distance < ZN)
            def _():
                tile_copy(z + distance, c, t, ag_send.at[0, c]).wait_recv()

                @pl.when(z - 1 >= 0)
                def _():
                    tile_copy(z + distance, c, t - 1, fw_send.at[z + distance, c]).start()

    def dispatch_copy(it, d):
        return pltpu.make_async_remote_copy(
            src_ref=disp.at[it, plane_peer(d)],
            dst_ref=recv.at[it, j],
            send_sem=xs.at[it],
            recv_sem=xr.at[it],
            device_id={"tile": plane_peer(d) * ZN + z},
            device_id_type=MESH,
        )

    def return_copy(it, d):
        return pltpu.make_async_remote_copy(
            src_ref=eout.at[it, plane_peer(d)],
            dst_ref=ret.at[it, j],
            send_sem=ys.at[it],
            recv_sem=yr.at[it],
            device_id={"tile": plane_peer(d) * ZN + z},
            device_id_type=MESH,
        )

    def all_of(src, dst, it, send_sem, recv_sem):
        return pltpu.make_async_remote_copy(
            src_ref=src.at[it, pl.ds(0, JN - 1)],
            dst_ref=dst.at[it, pl.ds(0, JN - 1)],
            send_sem=send_sem.at[it],
            recv_sem=recv_sem.at[it],
            device_id={"tile": t},
            device_id_type=MESH,
        )

    slots = JN * CAP
    slot_of = lax.broadcasted_iota(jnp.int32, (slots, rows), 0).astype(jnp.float32)

    def stage_dispatch(it):
        s = tile_order(z, it)
        base = (z * slots).astype(jnp.float32)
        meta = meta_all[s] - base
        picks = (slot_of == meta[0:1]) | (slot_of == meta[1:2])
        table = picks.astype(jnp.float32).astype(jnp.bfloat16)
        picked = jnp.dot(table, x_all[s], preferred_element_type=jnp.float32).astype(jnp.bfloat16)
        disp[it] = picked.reshape(JN, CAP, model)

        def start(d, carry):
            dispatch_copy(it, d).start()
            return carry

        lax.fori_loop(1, JN, start, 0)
        recv[it, j] = disp[it, j]

    def stage_expert(it):
        all_of(disp, recv, it, xs, xr).wait_recv()
        zrows = recv[it].reshape(slots, model)
        gate_part = jnp.dot(zrows, wg[...], preferred_element_type=jnp.float32)
        up_part = jnp.dot(zrows, wu[...], preferred_element_type=jnp.float32)
        hidden = (gate_part / (1.0 + jnp.exp(-gate_part)) * up_part).astype(jnp.bfloat16)
        result = jnp.dot(hidden, wd[...], preferred_element_type=jnp.float32)
        eout[it] = result.astype(jnp.bfloat16).reshape(JN, CAP, model)

        def start(d, carry):
            return_copy(it, d).start()
            return carry

        lax.fori_loop(1, JN, start, 0)
        ret[it, j] = eout[it, j]

    def rs_copy(it):
        s = tile_order(z, it)
        return pltpu.make_async_remote_copy(
            src_ref=rs_out.at[it],
            dst_ref=rs_in.at[z],
            send_sem=rs_send.at[it],
            recv_sem=rs_recv.at[z],
            device_id={"tile": j * ZN + s},
            device_id_type=MESH,
        )

    def stage_combine(it):
        all_of(eout, ret, it, ys, yr).wait_recv()
        s = tile_order(z, it)
        base = (z * slots).astype(jnp.float32)
        meta = meta_all[s]
        pos = meta[0:2] - base
        weights = jnp.where(slot_of == pos[0:1], meta[2:3], 0.0) + jnp.where(
            slot_of == pos[1:2], meta[3:4], 0.0
        )
        part = lax.dot_general(
            weights.astype(jnp.bfloat16),
            ret[it].reshape(slots, model),
            (((0,), (0,)), ((), ())),
            preferred_element_type=jnp.float32,
        )

        @pl.when(it == 0)
        def _():
            own[...] = part

        @pl.when(it > 0)
        def _():
            rs_out[it] = part.astype(jnp.bfloat16)
            rs_copy(it).start()

    for d in range(1, ZN):
        src = lax.rem(z + d, ZN)
        pltpu.make_async_remote_copy(
            src_ref=meta_own,
            dst_ref=meta_all.at[src],
            send_sem=meta_send.at[0],
            recv_sem=meta_recv.at[src],
            device_id={"tile": t},
            device_id_type=MESH,
        ).wait_recv()
    for c in late:
        c.wait()

    def each(stage):
        def body(n, carry):
            stage(n)
            return carry

        return body

    def step(it, carry):
        for distance in range(1, ZN):

            @pl.when(it == distance)
            def _():
                arrive(distance)

        @pl.when(it < ZN)
        def _():
            stage_dispatch(it)

        lax.fori_loop(
            jnp.where(it == 2, 0, it - 1), jnp.where(it < 2, it - 1, it), each(stage_combine), 0
        )
        lax.fori_loop(
            jnp.where(it == 1, 0, it),
            jnp.where((it > 0) & (it < ZN), it + 1, it),
            each(stage_expert),
            0,
        )
        return carry

    lax.fori_loop(0, ZN + 1, step, 0)

    total = own[...] + resid[...].astype(jnp.float32)
    for d in range(1, ZN):
        src = lax.rem(z + d, ZN)
        pltpu.make_async_remote_copy(
            src_ref=rs_out.at[0],
            dst_ref=rs_in.at[src],
            send_sem=rs_send.at[0],
            recv_sem=rs_recv.at[src],
            device_id={"tile": t},
            device_id_type=MESH,
        ).wait_recv()
        total = total + rs_in[src].astype(jnp.float32)
    out_ref[...] = total.astype(jnp.bfloat16)

    for d in range(1, ZN):
        send_meta(d).wait_send()

    for n in range(4):

        @pl.when(t < tiles - 1 if n < 2 else t > 0)
        def _():
            for kv in range(2):
                halo_copy(n, kv).wait_send()

    for c in range(len(chunks)):

        @pl.when(z < ZN - 1)
        def _():
            tile_copy(z, c, t, ag_send.at[0, c]).wait_send()

        @pl.when(z > 0)
        def _():
            tile_copy(z, c, t, ag_send.at[1, c]).wait_send()

        for distance in range(1, ZN):

            @pl.when((z - distance >= 0) & (z + 1 < ZN))
            def _():
                tile_copy(z - distance, c, t, fw_send.at[z - distance, c]).wait_send()

            @pl.when((z + distance < ZN) & (z - 1 >= 0))
            def _():
                tile_copy(z + distance, c, t, fw_send.at[z + distance, c]).wait_send()

    def drain(it, carry):
        all_of(disp, recv, it, xs, xr).wait_send()
        all_of(eout, ret, it, ys, yr).wait_send()

        @pl.when(it > 0)
        def _():
            rs_copy(it).wait_send()

        return carry

    lax.fori_loop(0, ZN, drain, 0)


def local(
    inputs,
    queries,
    key_vectors,
    values,
    out_weight,
    norm_gain,
    routes,
    route_gates,
    w_gate,
    w_up,
    w_down,
):
    rows, model = inputs.shape
    wide = w_gate.shape[2]
    plane = XL * DP
    halo = R_IL * plane
    bf16 = jnp.bfloat16
    f32 = jnp.float32
    vmem = pl.BlockSpec(memory_space=pltpu.VMEM)
    anywhere = pl.BlockSpec(memory_space=pl.ANY)
    dma = pltpu.SemaphoreType.DMA
    return pl.pallas_call(
        layer_kernel,
        out_shape=jax.ShapeDtypeStruct((rows, model), bf16),
        in_specs=[anywhere] * 5 + [vmem] * 3 + [anywhere] * 3,
        out_specs=vmem,
        scratch_shapes=[
            pltpu.VMEM((rows, model), bf16),
            pltpu.VMEM((rows, model), bf16),
            pltpu.VMEM((rows + 2 * halo, model), bf16),
            pltpu.VMEM((rows + 2 * halo, model), bf16),
            pltpu.VMEM((model, model), bf16),
            pltpu.VMEM((rows, model), bf16),
            pltpu.VMEM((4 * plane, (2 * R_IL + 1) * plane), f32),
            pltpu.VMEM((model, wide), bf16),
            pltpu.VMEM((model, wide), bf16),
            pltpu.VMEM((wide, model), bf16),
            pltpu.VMEM((8, rows), f32),
            pltpu.VMEM((ZN, 8, rows), f32),
            pltpu.VMEM((ZN, rows, model), bf16),
            pltpu.VMEM((rows, model), bf16),
            pltpu.VMEM((ZN, JN, CAP, model), bf16),
            pltpu.VMEM((ZN, JN, CAP, model), bf16),
            pltpu.VMEM((ZN, JN, CAP, model), bf16),
            pltpu.VMEM((ZN, JN, CAP, model), bf16),
            pltpu.VMEM((rows, model), f32),
            pltpu.VMEM((ZN, rows, model), bf16),
            pltpu.VMEM((ZN, rows, model), bf16),
            dma((8,)),
            dma((8,)),
            dma((8,)),
            dma((3,)),
            dma((ZN,)),
            dma((2, 3)),
            dma((ZN, 3)),
            dma((ZN, 3)),
            dma((ZN,)),
            dma((ZN,)),
            dma((ZN,)),
            dma((ZN,)),
            dma((ZN,)),
            dma((ZN,)),
        ],
        compiler_params=pltpu.CompilerParams(
            collective_id=1, has_side_effects=True, vmem_limit_bytes=58 * 1024 * 1024
        ),
    )(
        inputs,
        queries,
        key_vectors,
        values,
        out_weight,
        norm_gain.reshape(1, model),
        routes.T,
        route_gates.T,
        w_gate,
        w_up,
        w_down,
    )


def solution(mesh):
    return jax.shard_map(
        local,
        mesh=mesh,
        in_specs=(
            P(("rep", "tile"), None),
            P(("rep", "tile"), None),
            P(("rep", "tile"), None),
            P(("rep", "tile"), None),
            P(),
            P(),
            P(("rep", "tile"), None),
            P(("rep", "tile"), None),
            P("tile", None, None),
            P("tile", None, None),
            P("tile", None, None),
        ),
        out_specs=P(("rep", "tile"), None),
        check_vma=False,
    )
```

time: 165 us -> 130 us (0.79)
  the two profiles are of different devices: /device:TPU:64 before, /device:TPU:1 now
where the time goes in v2:
time: 130 us; the launch traced here: 129 us
  Pallas kernels  128 us (98%)
  local copies, waits for them, and re-layouts  1.87 us (1%)
    pallas_call x1, Pallas kernels, local(): pl.pallas_call(layer_kernel, out_shape=jax.ShapeDtypeStruct((rows, model)...  128 us

profile of v2, /device:TPU:1, one launch (start us, length us, event | category | flops | bytes accessed | tf_op | source)
XLA Modules:
  0.0 129.5 jit_solution(11285806767669400410)
XLA Ops:
  0.0 127.6 %shard_map.109 = bf16[256,1024]{1,0:T(8,128)(2,1)} custom-call(bf16[256,1024]{1,0:T(8,128)(2,1)} %x_hbm.1, bf16[256,1024]{1,0:T(8,128)(2,1)} %q_hbm.1, bf16[256,1024]{1,0:T(8,128)(2,1)} %k_hbm.1, bf16[256,1024]{1,0:T(8,128)(2,1)} %v_hbm.1, bf16[1024,1024]{1,0:T(8,128)(2,1)} %ow_hbm.1, f32[1,1024]{1,0:T(1,128)} %bitcast.3, s32[2,256]{1,0:T(2,128)} %bitcast.4, ...), custom_call_target="tpu_custom_call" | custom-call | tf_op jit(solution)/shard_map/pallas_call | solution.py:553
  127.6 1.9 %copy.13 = bf16[256,1024]{1,0:T(8,128)(2,1)} copy(bf16[256,1024]{1,0:T(8,128)(2,1)} %shard_map.109) | data formatting | bytes 1048576

commit v3 on v2

v3 whole, which is shorter than its diff:
```python
import jax
import jax.numpy as jnp
from jax import lax
from jax.experimental import pallas as pl
from jax.experimental.pallas import tpu as pltpu
from jax.sharding import PartitionSpec as P

HEADS = 16
HD = 64
IL_DEV = 4
XL = 8
DP = 8
R_IL = 2
R_XL = 2
R_DP = 2
ZN = 4
JN = 16
CAP = 8
PIECES = 2 * ZN
MESH = pl.DeviceIdType.MESH


def tile_order(z, it):
    low = jnp.where(z == 0, it, lax.rem(it + 1, ZN))
    mirrored = jnp.where(z == 3, it, lax.rem(it + 1, ZN))
    return jnp.where(z < 2, low, 3 - mirrored)


def layer_kernel(
    x_hbm,
    q_hbm,
    k_hbm,
    v_hbm,
    ow_hbm,
    gain_ref,
    routes_ref,
    gates_ref,
    wg_hbm,
    wu_hbm,
    wd_hbm,
    out_ref,
    x_in,
    q_in,
    ke,
    ve,
    ow,
    att,
    near,
    wg,
    wu,
    wd,
    meta_own,
    meta_all,
    x_all,
    resid,
    disp,
    recv,
    eout,
    ret,
    own,
    partial,
    rs_out,
    merge_in,
    final_in,
    l_sem,
    h_send,
    h_recv,
    meta_send,
    meta_recv,
    ag_send,
    fw_send,
    ag_recv,
    xs,
    xr,
    ys,
    yr,
    rs_send,
    merge_recv,
    final_recv,
):
    t = lax.axis_index("tile")
    tiles = lax.axis_size("tile")
    z = lax.rem(t, ZN)
    j = lax.div(t, ZN)
    rows = x_in.shape[0]
    model = x_in.shape[1]
    plane = XL * DP
    halo = R_IL * plane
    keys = (2 * R_IL + 1) * plane
    bf16 = jnp.bfloat16
    f32 = jnp.float32

    def local_copy(src, dst, n):
        return pltpu.make_async_copy(src, dst, l_sem.at[n])

    early = [
        local_copy(k_hbm, ke.at[pl.ds(halo, rows)], 0),
        local_copy(v_hbm, ve.at[pl.ds(halo, rows)], 1),
        local_copy(q_hbm, q_in, 2),
    ]
    mid = [local_copy(x_hbm, x_in, 3), local_copy(ow_hbm, ow, 4)]
    late = [
        local_copy(wg_hbm.at[0], wg, 5),
        local_copy(wu_hbm.at[0], wu, 6),
        local_copy(wd_hbm.at[0], wd, 7),
    ]

    barrier = pltpu.get_barrier_semaphore()

    def greet(tile):
        pl.semaphore_signal(barrier, inc=1, device_id={"tile": tile}, device_id_type=MESH)

    def z_peer(d):
        return j * ZN + lax.rem(z + d, ZN)

    def plane_peer(d):
        return lax.rem(j + d, JN)

    @pl.when(t > 0)
    def _():
        greet(t - 1)

    @pl.when(t < tiles - 1)
    def _():
        greet(t + 1)

    for d in range(1, ZN):
        greet(z_peer(d))

    def greet_plane(d, carry):
        greet(plane_peer(d) * ZN + z)
        return carry

    lax.fori_loop(1, JN, greet_plane, 0)
    for c in early + mid + late:
        c.start()
    pl.semaphore_wait(
        barrier,
        JN - 1 + ZN - 1 + jnp.where(t > 0, 1, 0) + jnp.where(t < tiles - 1, 1, 0),
    )

    def halo_copy(n, kv):
        src, dst = ((rows - halo, 0), (0, halo + rows))[n]
        return pltpu.make_async_remote_copy(
            src_ref=(k_hbm, v_hbm)[kv].at[pl.ds(src, halo)],
            dst_ref=(ke, ve)[kv].at[pl.ds(dst, halo)],
            send_sem=h_send.at[2 * n + kv],
            recv_sem=h_recv.at[2 * n + kv],
            device_id={"tile": t + 1 if n == 0 else t - 1},
            device_id_type=MESH,
        )

    @pl.when(t < tiles - 1)
    def _():
        for kv in range(2):
            halo_copy(0, kv).start()

    @pl.when(t == 0)
    def _():
        ke[0:halo] = jnp.zeros((halo, model), bf16)
        ve[0:halo] = jnp.zeros((halo, model), bf16)

    @pl.when(t == tiles - 1)
    def _():
        ke[halo + rows :] = jnp.zeros((halo, model), bf16)
        ve[halo + rows :] = jnp.zeros((halo, model), bf16)

    def halo_wait(n):
        @pl.when(t > 0 if n == 0 else t < tiles - 1)
        def _():
            for kv in range(2):
                halo_copy(n, kv).wait_recv()

    block = rows // 2
    ti = lax.broadcasted_iota(jnp.int32, (rows, rows), 0)
    tj = lax.broadcasted_iota(jnp.int32, (rows, rows), 1)
    same = ti == tj
    before = (ti < tj) & ((ti < block) == (tj < block))
    route = routes_ref[...].astype(f32)
    cols = [
        jnp.sum(jnp.where(same, route[k : k + 1], 0.0), axis=1, keepdims=True) for k in range(2)
    ]
    for k in range(2):
        r = route[k : k + 1]
        hits = jnp.where(cols[0] == r, 1.0, 0.0) + jnp.where(cols[1] == r, 1.0, 0.0)
        rank = jnp.sum(jnp.where(before, hits, 0.0), axis=0, keepdims=True)
        column = jnp.floor(r * (1.0 / ZN))
        meta_own[k : k + 1, :] = (r - ZN * column) * (JN * CAP) + column * CAP + rank
    meta_own[2:4, :] = gates_ref[...]
    meta_own[4:8, :] = jnp.zeros((4, rows), f32)

    def send_meta(d):
        return pltpu.make_async_remote_copy(
            src_ref=meta_own,
            dst_ref=meta_all.at[z],
            send_sem=meta_send.at[d - 1],
            recv_sem=meta_recv.at[z],
            device_id={"tile": z_peer(d)},
            device_id_type=MESH,
        )

    for d in range(1, ZN):
        send_meta(d).start()
    meta_all[z] = meta_own[...]

    @pl.when(t < tiles - 1)
    def _():
        for kv in range(2):
            halo_copy(0, kv).wait_send()

    @pl.when(t > 0)
    def _():
        for kv in range(2):
            halo_copy(1, kv).start()

    qi = lax.rem(lax.broadcasted_iota(jnp.int32, (4 * plane, keys), 0), plane)
    ki = lax.broadcasted_iota(jnp.int32, (4 * plane, keys), 1)
    kp = lax.rem(ki, plane)
    close = (jnp.abs(lax.div(qi, DP) - lax.div(kp, DP)) <= R_XL) & (
        jnp.abs(lax.rem(qi, DP) - lax.rem(kp, DP)) <= R_DP
    )
    near[...] = jnp.where(close, 0.0, -1e30)
    kcol = lax.div(lax.broadcasted_iota(jnp.int32, (1, keys), 1), plane)
    lane_head = lax.div(lax.broadcasted_iota(jnp.int32, (plane, 4 * HD), 1), HD)

    def attend(i):
        outside = ((t == 0) & (kcol < R_IL - i)) | (
            (t == tiles - 1) & (kcol > IL_DEV - 1 + R_IL - i)
        )
        bias = near[...] + jnp.where(outside, -1e30, 0.0)
        for g in range(HEADS // 4):
            lanes = slice(g * 4 * HD, (g + 1) * 4 * HD)
            q4 = q_in[i * plane : (i + 1) * plane, lanes].astype(f32) * (1.0 / HD**0.5)
            stacked = jnp.concatenate(
                [jnp.where(lane_head == h, q4, 0.0).astype(bf16) for h in range(4)], axis=0
            )
            window = slice(i * plane, i * plane + keys)
            scores = lax.dot_general(
                stacked,
                ke[window, lanes],
                (((1,), (1,)), ((), ())),
                preferred_element_type=f32,
            )
            scores = scores + bias
            highest = jnp.max(scores, axis=1, keepdims=True)
            weights = jnp.exp(scores - highest)
            totals = jnp.sum(weights, axis=1, keepdims=True)
            probs = (weights * (1.0 / totals)).astype(bf16)
            mixed = jnp.dot(probs, ve[window, lanes], preferred_element_type=f32)
            picked = mixed[0:plane]
            for h in range(1, 4):
                picked = jnp.where(lane_head == h, mixed[h * plane : (h + 1) * plane], picked)
            att[i * plane : (i + 1) * plane, lanes] = picked.astype(bf16)

    def finish(h):
        part = slice(h * block, (h + 1) * block)
        sums = x_in[part].astype(f32) + jnp.dot(att[part], ow[...], preferred_element_type=f32)
        rounded = sums.astype(bf16)
        wide = rounded.astype(f32)
        mean_square = jnp.mean(wide * wide, axis=1, keepdims=True)
        resid[part] = rounded
        x_all[z, part] = (wide * lax.rsqrt(mean_square + 1e-06) * gain_ref[...]).astype(bf16)

    def tile_copy(slot, h, to, send_sem):
        part = pl.ds(pl.multiple_of(h * block, block), block)
        return pltpu.make_async_remote_copy(
            src_ref=x_all.at[slot, part],
            dst_ref=x_all.at[slot, part],
            send_sem=send_sem,
            recv_sem=ag_recv.at[slot, h],
            device_id={"tile": to},
            device_id_type=MESH,
        )

    def send_own(c):
        @pl.when(z < ZN - 1)
        def _():
            tile_copy(z, c, t + 1, ag_send.at[0, c]).start()

        @pl.when(z > 0)
        def _():
            tile_copy(z, c, t - 1, ag_send.at[1, c]).start()

    def arrive(distance, h):
        @pl.when(z - distance >= 0)
        def _():
            tile_copy(z - distance, h, t, ag_send.at[0, h]).wait_recv()

            @pl.when(z + 1 < ZN)
            def _():
                tile_copy(z - distance, h, t + 1, fw_send.at[z - distance, h]).start()

        @pl.when(z + distance < ZN)
        def _():
            tile_copy(z + distance, h, t, ag_send.at[0, h]).wait_recv()

            @pl.when(z - 1 >= 0)
            def _():
                tile_copy(z + distance, h, t - 1, fw_send.at[z + distance, h]).start()

    def dispatch_copy(m, d):
        return pltpu.make_async_remote_copy(
            src_ref=disp.at[m, plane_peer(d)],
            dst_ref=recv.at[m, j],
            send_sem=xs.at[m],
            recv_sem=xr.at[m],
            device_id={"tile": plane_peer(d) * ZN + z},
            device_id_type=MESH,
        )

    def return_copy(m, d):
        return pltpu.make_async_remote_copy(
            src_ref=eout.at[m, plane_peer(d)],
            dst_ref=ret.at[m, j],
            send_sem=ys.at[m],
            recv_sem=yr.at[m],
            device_id={"tile": plane_peer(d) * ZN + z},
            device_id_type=MESH,
        )

    def all_of(src, dst, m, send_sem, recv_sem):
        return pltpu.make_async_remote_copy(
            src_ref=src.at[m, pl.ds(0, JN - 1)],
            dst_ref=dst.at[m, pl.ds(0, JN - 1)],
            send_sem=send_sem.at[m],
            recv_sem=recv_sem.at[m],
            device_id={"tile": t},
            device_id_type=MESH,
        )

    slots = JN * CAP
    slot_of = lax.broadcasted_iota(jnp.int32, (slots, block), 0).astype(f32)
    end = (z == 0) | (z == ZN - 1)
    inward = jnp.where(z < 2, 1, -1)

    def piece_meta(m):
        h = lax.rem(m, 2)
        meta = meta_all[tile_order(z, lax.div(m, 2))]
        meta = jnp.where(h == 0, meta[:, 0:block], meta[:, block:])
        return meta[0:2] - (z * slots).astype(f32), meta[2:4]

    def stage_dispatch(m):
        s = tile_order(z, lax.div(m, 2))
        pos, _ = piece_meta(m)
        table = jnp.where((slot_of == pos[0:1]) | (slot_of == pos[1:2]), 1.0, 0.0).astype(bf16)
        part = pl.ds(pl.multiple_of(lax.rem(m, 2) * block, block), block)
        picked = jnp.dot(table, x_all[s, part], preferred_element_type=f32)
        disp[m] = picked.reshape(JN, CAP, model).astype(bf16)

        def start(d, carry):
            dispatch_copy(m, d).start()
            return carry

        lax.fori_loop(1, JN, start, 0)
        recv[m, j] = disp[m, j]

    def stage_expert(m):
        all_of(disp, recv, m, xs, xr).wait_recv()
        zrows = recv[m].astype(f32).reshape(slots, model).astype(bf16)
        gate_part = jnp.dot(zrows, wg[...], preferred_element_type=f32)
        up_part = jnp.dot(zrows, wu[...], preferred_element_type=f32)
        hidden = (gate_part / (1.0 + jnp.exp(-gate_part)) * up_part).astype(bf16)
        result = jnp.dot(hidden, wd[...], preferred_element_type=f32)
        eout[m] = result.reshape(JN, CAP, model).astype(bf16)

        def start(d, carry):
            return_copy(m, d).start()
            return carry

        lax.fori_loop(1, JN, start, 0)
        ret[m, j] = eout[m, j]

    def sum_copy(m, dst, recv_sem, to):
        return pltpu.make_async_remote_copy(
            src_ref=rs_out.at[m],
            dst_ref=dst,
            send_sem=rs_send.at[m],
            recv_sem=recv_sem,
            device_id={"tile": to},
            device_id_type=MESH,
        )

    def to_merge(m, h):
        kind = jnp.where(end, 0, 1)
        return sum_copy(m, merge_in.at[kind, h], merge_recv.at[kind, h], t + inward)

    def to_final(m, h, side):
        s = tile_order(z, lax.div(m, 2))
        return sum_copy(m, final_in.at[side, h], final_recv.at[side, h], j * ZN + s)

    def next_side(m):
        return jnp.where(z < tile_order(z, lax.div(m, 2)), 0, 1)

    def stage_combine(m):
        all_of(eout, ret, m, ys, yr).wait_recv()
        it = lax.div(m, 2)
        h = lax.rem(m, 2)
        pos, gate = piece_meta(m)
        weights = jnp.where(slot_of == pos[0:1], gate[0:1], 0.0) + jnp.where(
            slot_of == pos[1:2], gate[1:2], 0.0
        )
        part = lax.dot_general(
            weights.astype(bf16),
            ret[m].astype(f32).reshape(slots, model).astype(bf16),
            (((0,), (0,)), ((), ())),
            preferred_element_type=f32,
        )

        @pl.when(it == 0)
        def _():
            own[pl.ds(pl.multiple_of(h * block, block), block)] = part

        @pl.when((it == 1) & end)
        def _():
            rs_out[m] = part.astype(bf16)
            to_final(m, h, next_side(m)).start()

        @pl.when((it == 1) & ~end)
        def _():
            partial[h] = part

        @pl.when(it == 2)
        def _():
            rs_out[m] = part.astype(bf16)
            to_merge(m, h).start()

        @pl.when((it == 3) & end)
        def _():
            rs_out[m] = part.astype(bf16)
            to_final(m, h, 2).start()

        @pl.when((it == 3) & ~end)
        def _():
            sum_copy(m, merge_in.at[1, h], merge_recv.at[1, h], t).wait_recv()
            rs_out[m] = (part + merge_in[1, h].astype(f32)).astype(bf16)
            to_final(m, h, next_side(m)).start()

    def stage_merge(m):
        h = lax.rem(m, 2)

        @pl.when(~end)
        def _():
            sum_copy(m, merge_in.at[0, h], merge_recv.at[0, h], t).wait_recv()
            rs_out[m] = (partial[h] + merge_in[0, h].astype(f32)).astype(bf16)
            to_final(m, h, next_side(m)).start()

    for c in early:
        c.wait()
    halo_wait(0)
    attend(0)
    attend(1)
    for c in mid:
        c.wait()
    finish(0)
    send_own(0)
    for d in range(1, ZN):
        src = lax.rem(z + d, ZN)
        pltpu.make_async_remote_copy(
            src_ref=meta_own,
            dst_ref=meta_all.at[src],
            send_sem=meta_send.at[0],
            recv_sem=meta_recv.at[src],
            device_id={"tile": t},
            device_id_type=MESH,
        ).wait_recv()
    for c in late:
        c.wait()
    halo_wait(1)
    attend(2)
    attend(3)
    finish(1)
    send_own(1)

    def step(k, carry):
        for distance in range(1, ZN):

            @pl.when(lax.div(k, 2) == distance)
            def _():
                arrive(distance, lax.rem(k, 2))

        @pl.when(k < PIECES)
        def _():
            stage_dispatch(k)

        @pl.when((k >= 1) & (k < PIECES + 1))
        def _():
            stage_expert(k - 1)

        @pl.when(k >= 2)
        def _():
            stage_combine(k - 2)

        @pl.when((k == 7) | (k == 8))
        def _():
            stage_merge(k - 5)

        return carry

    lax.fori_loop(0, PIECES + 2, step, 0)

    def add_final(side, h):
        sum_copy(0, final_in.at[side, h], final_recv.at[side, h], t).wait_recv()
        part = slice(h * block, (h + 1) * block)
        own[part] = own[part] + final_in[side, h].astype(f32)

    for h in range(2):

        @pl.when(z > 0)
        def _():
            add_final(0, h)

        @pl.when(z < ZN - 1)
        def _():
            add_final(1, h)

        @pl.when(end)
        def _():
            add_final(2, h)

        part = slice(h * block, (h + 1) * block)
        out_ref[part] = (own[part] + resid[part].astype(f32)).astype(bf16)

    for d in range(1, ZN):
        send_meta(d).wait_send()

    @pl.when(t > 0)
    def _():
        for kv in range(2):
            halo_copy(1, kv).wait_send()

    for h in range(2):

        @pl.when(z < ZN - 1)
        def _():
            tile_copy(z, h, t, ag_send.at[0, h]).wait_send()

        @pl.when(z > 0)
        def _():
            tile_copy(z, h, t, ag_send.at[1, h]).wait_send()

        for distance in range(1, ZN):

            @pl.when((z - distance >= 0) & (z + 1 < ZN))
            def _():
                tile_copy(z - distance, h, t, fw_send.at[z - distance, h]).wait_send()

            @pl.when((z + distance < ZN) & (z - 1 >= 0))
            def _():
                tile_copy(z + distance, h, t, fw_send.at[z + distance, h]).wait_send()

    def drain(m, carry):
        all_of(disp, recv, m, xs, xr).wait_send()
        all_of(eout, ret, m, ys, yr).wait_send()

        @pl.when(m >= 2)
        def _():
            sum_copy(m, final_in.at[0, 0], final_recv.at[0, 0], t).wait_send()

        return carry

    lax.fori_loop(0, PIECES, drain, 0)


def local(
    inputs,
    queries,
    key_vectors,
    values,
    out_weight,
    norm_gain,
    routes,
    route_gates,
    w_gate,
    w_up,
    w_down,
):
    rows, model = inputs.shape
    wide = w_gate.shape[2]
    plane = XL * DP
    halo = R_IL * plane
    bf16 = jnp.bfloat16
    f32 = jnp.float32
    vmem = pl.BlockSpec(memory_space=pltpu.VMEM)
    anywhere = pl.BlockSpec(memory_space=pl.ANY)
    dma = pltpu.SemaphoreType.DMA
    return pl.pallas_call(
        layer_kernel,
        out_shape=jax.ShapeDtypeStruct((rows, model), bf16),
        in_specs=[anywhere] * 5 + [vmem] * 3 + [anywhere] * 3,
        out_specs=vmem,
        scratch_shapes=[
            pltpu.VMEM((rows, model), bf16),
            pltpu.VMEM((rows, model), bf16),
            pltpu.VMEM((rows + 2 * halo, model), bf16),
            pltpu.VMEM((rows + 2 * halo, model), bf16),
            pltpu.VMEM((model, model), bf16),
            pltpu.VMEM((rows, model), bf16),
            pltpu.VMEM((4 * plane, (2 * R_IL + 1) * plane), f32),
            pltpu.VMEM((model, wide), bf16),
            pltpu.VMEM((model, wide), bf16),
            pltpu.VMEM((wide, model), bf16),
            pltpu.VMEM((8, rows), f32),
            pltpu.VMEM((ZN, 8, rows), f32),
            pltpu.VMEM((ZN, rows, model), bf16),
            pltpu.VMEM((rows, model), bf16),
            pltpu.VMEM((PIECES, JN, CAP, model), bf16),
            pltpu.VMEM((PIECES, JN, CAP, model), bf16),
            pltpu.VMEM((PIECES, JN, CAP, model), bf16),
            pltpu.VMEM((PIECES, JN, CAP, model), bf16),
            pltpu.VMEM((rows, model), f32),
            pltpu.VMEM((2, rows // 2, model), f32),
            pltpu.VMEM((PIECES, rows // 2, model), bf16),
            pltpu.VMEM((2, 2, rows // 2, model), bf16),
            pltpu.VMEM((3, 2, rows // 2, model), bf16),
            dma((8,)),
            dma((4,)),
            dma((4,)),
            dma((3,)),
            dma((ZN,)),
            dma((2, 2)),
            dma((ZN, 2)),
            dma((ZN, 2)),
            dma((PIECES,)),
            dma((PIECES,)),
            dma((PIECES,)),
            dma((PIECES,)),
            dma((PIECES,)),
            dma((2, 2)),
            dma((3, 2)),
        ],
        compiler_params=pltpu.CompilerParams(
            collective_id=1, has_side_effects=True, vmem_limit_bytes=58 * 1024 * 1024
        ),
    )(
        inputs,
        queries,
        key_vectors,
        values,
        out_weight,
        norm_gain.reshape(1, model),
        routes.T,
        route_gates.T,
        w_gate,
        w_up,
        w_down,
    )


def solution(mesh):
    return jax.shard_map(
        local,
        mesh=mesh,
        in_specs=(
            P(("rep", "tile"), None),
            P(("rep", "tile"), None),
            P(("rep", "tile"), None),
            P(("rep", "tile"), None),
            P(),
            P(),
            P(("rep", "tile"), None),
            P(("rep", "tile"), None),
            P("tile", None, None),
            P("tile", None, None),
            P("tile", None, None),
        ),
        out_specs=P(("rep", "tile"), None),
        check_vma=False,
    )
```

time: 130 us -> 109 us (0.84)
  the two profiles are of different devices: /device:TPU:1 before, /device:TPU:64 now
where the time goes in v3:
time: 109 us
  Pallas kernels  107 us (98%)
  local copies, waits for them, and re-layouts  1.87 us (2%)
    pallas_call x1, Pallas kernels, local(): pl.pallas_call(layer_kernel, out_shape=jax.ShapeDtypeStruct((rows, model)...  107 us

profile of v3, /device:TPU:64, one launch (start us, length us, event | category | flops | bytes accessed | tf_op | source)
XLA Modules:
  0.0 108.9 jit_solution(7639850616089260511)
XLA Ops:
  0.0 107.0 %shard_map.109 = bf16[256,1024]{1,0:T(8,128)(2,1)} custom-call(bf16[256,1024]{1,0:T(8,128)(2,1)} %x_hbm.1, bf16[256,1024]{1,0:T(8,128)(2,1)} %q_hbm.1, bf16[256,1024]{1,0:T(8,128)(2,1)} %k_hbm.1, bf16[256,1024]{1,0:T(8,128)(2,1)} %v_hbm.1, bf16[1024,1024]{1,0:T(8,128)(2,1)} %ow_hbm.1, f32[1,1024]{1,0:T(1,128)} %bitcast.3, s32[2,256]{1,0:T(2,128)} %bitcast.4, ...), custom_call_target="tpu_custom_call" | custom-call | tf_op jit(solution)/shard_map/pallas_call | solution.py:586
  107.0 1.9 %copy.13 = bf16[256,1024]{1,0:T(8,128)(2,1)} copy(bf16[256,1024]{1,0:T(8,128)(2,1)} %shard_map.109) | data formatting | bytes 1048576

commit v4 on v3

--- a/solution.py
+++ b/solution.py
@@ -18,12 +18,6 @@
 CAP = 8
 PIECES = 2 * ZN
 MESH = pl.DeviceIdType.MESH
-
-
-def tile_order(z, it):
-    low = jnp.where(z == 0, it, lax.rem(it + 1, ZN))
-    mirrored = jnp.where(z == 3, it, lax.rem(it + 1, ZN))
-    return jnp.where(z < 2, low, 3 - mirrored)
 
 
 def layer_kernel(
@@ -203,14 +197,14 @@
         send_meta(d).start()
     meta_all[z] = meta_own[...]
 
-    @pl.when(t < tiles - 1)
-    def _():
-        for kv in range(2):
+    for kv in range(2):
+
+        @pl.when(t < tiles - 1)
+        def _():
             halo_copy(0, kv).wait_send()
 
-    @pl.when(t > 0)
-    def _():
-        for kv in range(2):
+        @pl.when(t > 0)
+        def _():
             halo_copy(1, kv).start()
 
     qi = lax.rem(lax.broadcasted_iota(jnp.int32, (4 * plane, keys), 0), plane)
@@ -272,31 +266,64 @@
             device_id_type=MESH,
         )
 
-    def send_own(c):
-        @pl.when(z < ZN - 1)
-        def _():
-            tile_copy(z, c, t + 1, ag_send.at[0, c]).start()
-
-        @pl.when(z > 0)
-        def _():
-            tile_copy(z, c, t - 1, ag_send.at[1, c]).start()
-
-    def arrive(distance, h):
-        @pl.when(z - distance >= 0)
-        def _():
-            tile_copy(z - distance, h, t, ag_send.at[0, h]).wait_recv()
-
-            @pl.when(z + 1 < ZN)
-            def _():
-                tile_copy(z - distance, h, t + 1, fw_send.at[z - distance, h]).start()
-
-        @pl.when(z + distance < ZN)
-        def _():
-            tile_copy(z + distance, h, t, ag_send.at[0, h]).wait_recv()
-
-            @pl.when(z - 1 >= 0)
-            def _():
-                tile_copy(z + distance, h, t - 1, fw_send.at[z + distance, h]).start()
+    end = (z == 0) | (z == ZN - 1)
+    inward = jnp.where(z < 2, 1, -1)
+    t_in = t + inward
+    t_out = jnp.where(end, t, t - inward)
+    in1 = z + inward
+    in2 = z + 2 * inward
+    out1 = jnp.where(end, z, z - inward)
+
+    def own_in(h):
+        return tile_copy(z, h, t_in, ag_send.at[0, h])
+
+    def own_out(h):
+        return tile_copy(z, h, t_out, ag_send.at[1, h])
+
+    def forward(slot, h, to):
+        return tile_copy(slot, h, to, fw_send.at[slot, h])
+
+    def arrived(slot, h):
+        tile_copy(slot, h, t_in, ag_send.at[0, h]).wait_recv()
+
+    def piece(m):
+        h = jnp.where((m == 1) | (m >= 5), 1, 0)
+        at_end = jnp.where(m < 2, 0, jnp.where(m < 5, m - 1, 8 - m))
+        at_mid = jnp.where((m == 4) | (m == 6), -1, jnp.where((m == 3) | (m == 5), 2, 1))
+        at_mid = jnp.where(m < 2, 0, at_mid)
+        return z + inward * jnp.where(end, at_end, at_mid), h
+
+    def arrive(k):
+        @pl.when(end & (k >= 2) & (k < PIECES))
+        def _():
+            slot, h = piece(k)
+            arrived(slot, h)
+
+        @pl.when(~end & (k == 2))
+        def _():
+            arrived(in1, 0)
+            forward(in1, 0, t_out).start()
+            arrived(out1, 0)
+            forward(out1, 0, t_in).start()
+
+        @pl.when(~end & (k == 3))
+        def _():
+            arrived(out1, 1)
+            forward(out1, 1, t_in).start()
+            own_in(1).start()
+            arrived(in2, 0)
+            forward(in2, 0, t_out).start()
+
+        @pl.when(~end & (k == 5))
+        def _():
+            arrived(in2, 1)
+            forward(in2, 1, t_out).start()
+
+        @pl.when(~end & (k == 7))
+        def _():
+            arrived(in1, 1)
+            forward(in1, 1, t_out).start()
+            own_out(1).start()
 
     def dispatch_copy(m, d):
         return pltpu.make_async_remote_copy(
@@ -330,20 +357,18 @@
 
     slots = JN * CAP
     slot_of = lax.broadcasted_iota(jnp.int32, (slots, block), 0).astype(f32)
-    end = (z == 0) | (z == ZN - 1)
-    inward = jnp.where(z < 2, 1, -1)
 
     def piece_meta(m):
-        h = lax.rem(m, 2)
-        meta = meta_all[tile_order(z, lax.div(m, 2))]
+        s, h = piece(m)
+        meta = meta_all[s]
         meta = jnp.where(h == 0, meta[:, 0:block], meta[:, block:])
         return meta[0:2] - (z * slots).astype(f32), meta[2:4]
 
     def stage_dispatch(m):
-        s = tile_order(z, lax.div(m, 2))
+        s, h = piece(m)
         pos, _ = piece_meta(m)
         table = jnp.where((slot_of == pos[0:1]) | (slot_of == pos[1:2]), 1.0, 0.0).astype(bf16)
-        part = pl.ds(pl.multiple_of(lax.rem(m, 2) * block, block), block)
+        part = pl.ds(pl.multiple_of(h * block, block), block)
         picked = jnp.dot(table, x_all[s, part], preferred_element_type=f32)
         disp[m] = picked.reshape(JN, CAP, model).astype(bf16)
 
@@ -382,19 +407,15 @@
 
     def to_merge(m, h):
         kind = jnp.where(end, 0, 1)
-        return sum_copy(m, merge_in.at[kind, h], merge_recv.at[kind, h], t + inward)
-
-    def to_final(m, h, side):
-        s = tile_order(z, lax.div(m, 2))
+        return sum_copy(m, merge_in.at[kind, h], merge_recv.at[kind, h], t_in)
+
+    def to_final(m, s, h):
+        side = jnp.where(end & ((m == 4) | (m == 5)), 2, jnp.where(z < s, 0, 1))
         return sum_copy(m, final_in.at[side, h], final_recv.at[side, h], j * ZN + s)
-
-    def next_side(m):
-        return jnp.where(z < tile_order(z, lax.div(m, 2)), 0, 1)
 
     def stage_combine(m):
         all_of(eout, ret, m, ys, yr).wait_recv()
-        it = lax.div(m, 2)
-        h = lax.rem(m, 2)
+        s, h = piece(m)
         pos, gate = piece_meta(m)
         weights = jnp.where(slot_of == pos[0:1], gate[0:1], 0.0) + jnp.where(
             slot_of == pos[1:2], gate[1:2], 0.0
@@ -406,43 +427,41 @@
             preferred_element_type=f32,
         )
 
-        @pl.when(it == 0)
+        @pl.when(m < 2)
         def _():
             own[pl.ds(pl.multiple_of(h * block, block), block)] = part
 
-        @pl.when((it == 1) & end)
+        @pl.when(end & ((m == 2) | (m == 4) | (m == 5) | (m == 7)))
         def _():
             rs_out[m] = part.astype(bf16)
-            to_final(m, h, next_side(m)).start()
-
-        @pl.when((it == 1) & ~end)
-        def _():
-            partial[h] = part
-
-        @pl.when(it == 2)
+            to_final(m, s, h).start()
+
+        @pl.when((m == 3) | (end & (m == 6)) | (~end & (m == 5)))
         def _():
             rs_out[m] = part.astype(bf16)
             to_merge(m, h).start()
 
-        @pl.when((it == 3) & end)
-        def _():
-            rs_out[m] = part.astype(bf16)
-            to_final(m, h, 2).start()
-
-        @pl.when((it == 3) & ~end)
-        def _():
-            sum_copy(m, merge_in.at[1, h], merge_recv.at[1, h], t).wait_recv()
-            rs_out[m] = (part + merge_in[1, h].astype(f32)).astype(bf16)
-            to_final(m, h, next_side(m)).start()
-
-    def stage_merge(m):
-        h = lax.rem(m, 2)
-
-        @pl.when(~end)
-        def _():
-            sum_copy(m, merge_in.at[0, h], merge_recv.at[0, h], t).wait_recv()
-            rs_out[m] = (partial[h] + merge_in[0, h].astype(f32)).astype(bf16)
-            to_final(m, h, next_side(m)).start()
+        @pl.when(~end & (m == 2))
+        def _():
+            partial[...] = part
+
+        def merge(kind):
+            sum_copy(m, merge_in.at[kind, h], merge_recv.at[kind, h], t).wait_recv()
+            rs_out[m] = (part + merge_in[kind, h].astype(f32)).astype(bf16)
+            to_final(m, s, h).start()
+
+        @pl.when(~end & ((m == 4) | (m == 6)))
+        def _():
+            merge(1)
+
+        @pl.when(~end & (m == 7))
+        def _():
+            merge(0)
+
+    def late_merge():
+        sum_copy(2, merge_in.at[0, 0], merge_recv.at[0, 0], t).wait_recv()
+        rs_out[2] = (partial[...] + merge_in[0, 0].astype(f32)).astype(bf16)
+        to_final(2, in1, 0).start()
 
     for c in early:
         c.wait()
@@ -452,7 +471,12 @@
     for c in mid:
         c.wait()
     finish(0)
-    send_own(0)
+    own_in(0).start()
+
+    @pl.when(~end)
+    def _():
+        own_out(0).start()
+
     for d in range(1, ZN):
         src = lax.rem(z + d, ZN)
         pltpu.make_async_remote_copy(
@@ -469,14 +493,13 @@
     attend(2)
     attend(3)
     finish(1)
-    send_own(1)
+
+    @pl.when(end)
+    def _():
+        own_in(1).start()
 
     def step(k, carry):
-        for distance in range(1, ZN):
-
-            @pl.when(lax.div(k, 2) == distance)
-            def _():
-                arrive(distance, lax.rem(k, 2))
+        arrive(k)
 
         @pl.when(k < PIECES)
         def _():
@@ -490,9 +513,9 @@
         def _():
             stage_combine(k - 2)
 
-        @pl.when((k == 7) | (k == 8))
-        def _():
-            stage_merge(k - 5)
+        @pl.when(~end & (k == 7))
+        def _():
+            late_merge()
 
         return carry
 
@@ -529,24 +552,13 @@
             halo_copy(1, kv).wait_send()
 
     for h in range(2):
-
-        @pl.when(z < ZN - 1)
-        def _():
-            tile_copy(z, h, t, ag_send.at[0, h]).wait_send()
-
-        @pl.when(z > 0)
-        def _():
-            tile_copy(z, h, t, ag_send.at[1, h]).wait_send()
-
-        for distance in range(1, ZN):
-
-            @pl.when((z - distance >= 0) & (z + 1 < ZN))
-            def _():
-                tile_copy(z - distance, h, t, fw_send.at[z - distance, h]).wait_send()
-
-            @pl.when((z + distance < ZN) & (z - 1 >= 0))
-            def _():
-                tile_copy(z + distance, h, t, fw_send.at[z + distance, h]).wait_send()
+        own_in(h).wait_send()
+
+        @pl.when(~end)
+        def _():
+            own_out(h).wait_send()
+            for slot in (in1, in2, out1):
+                forward(slot, h, t_in).wait_send()
 
     def drain(m, carry):
         all_of(disp, recv, m, xs, xr).wait_send()
@@ -608,7 +620,7 @@
             pltpu.VMEM((PIECES, JN, CAP, model), bf16),
             pltpu.VMEM((PIECES, JN, CAP, model), bf16),
             pltpu.VMEM((rows, model), f32),
-            pltpu.VMEM((2, rows // 2, model), f32),
+            pltpu.VMEM((rows // 2, model), f32),
             pltpu.VMEM((PIECES, rows // 2, model), bf16),
             pltpu.VMEM((2, 2, rows // 2, model), bf16),
             pltpu.VMEM((3, 2, rows // 2, model), bf16),

time: 109 us -> 120 us (1.10)
  Pallas kernels: 107 us -> 117 us
    pallas_call x1, Pallas kernels: 107 us -> 117 us  [local(): pl.pallas_call(layer_kernel, out_shape=jax.ShapeDtypeStruct((rows, model)...]
where the time goes in v4:
time: 120 us; the launch traced here: 119 us
  Pallas kernels  117 us (98%)
  local copies, waits for them, and re-layouts  1.87 us (2%)
    pallas_call x1, Pallas kernels, local(): pl.pallas_call(layer_kernel, out_shape=jax.ShapeDtypeStruct((rows, model)...  117 us

profile of v4, /device:TPU:64, one launch (start us, length us, event | category | flops | bytes accessed | tf_op | source)
XLA Modules:
  0.0 119.3 jit_solution(3440174284850468052)
XLA Ops:
  0.0 117.4 %shard_map.109 = bf16[256,1024]{1,0:T(8,128)(2,1)} custom-call(bf16[256,1024]{1,0:T(8,128)(2,1)} %x_hbm.1, bf16[256,1024]{1,0:T(8,128)(2,1)} %q_hbm.1, bf16[256,1024]{1,0:T(8,128)(2,1)} %k_hbm.1, bf16[256,1024]{1,0:T(8,128)(2,1)} %v_hbm.1, bf16[1024,1024]{1,0:T(8,128)(2,1)} %ow_hbm.1, f32[1,1024]{1,0:T(1,128)} %bitcast.3, s32[2,256]{1,0:T(2,128)} %bitcast.4, ...), custom_call_target="tpu_custom_call" | custom-call | tf_op jit(solution)/shard_map/pallas_call | solution.py:598
  117.4 1.9 %copy.13 = bf16[256,1024]{1,0:T(8,128)(2,1)} copy(bf16[256,1024]{1,0:T(8,128)(2,1)} %shard_map.109) | data formatting | bytes 1048576

commit v5 on v4

--- a/solution.py
+++ b/solution.py
@@ -107,8 +107,7 @@
     def z_peer(d):
         return j * ZN + lax.rem(z + d, ZN)
 
-    def plane_peer(d):
-        return lax.rem(j + d, JN)
+    peers = [lax.rem(j + d, JN) for d in range(JN)]
 
     @pl.when(t > 0)
     def _():
@@ -121,11 +120,8 @@
     for d in range(1, ZN):
         greet(z_peer(d))
 
-    def greet_plane(d, carry):
-        greet(plane_peer(d) * ZN + z)
-        return carry
-
-    lax.fori_loop(1, JN, greet_plane, 0)
+    for d in range(1, JN):
+        greet(peers[d] * ZN + z)
     for c in early + mid + late:
         c.start()
     pl.semaphore_wait(
@@ -299,14 +295,15 @@
             slot, h = piece(k)
             arrived(slot, h)
 
-        @pl.when(~end & (k == 2))
+    def pass_on(k):
+        @pl.when(~end & (k == 1))
         def _():
             arrived(in1, 0)
             forward(in1, 0, t_out).start()
             arrived(out1, 0)
             forward(out1, 0, t_in).start()
 
-        @pl.when(~end & (k == 3))
+        @pl.when(~end & (k == 2))
         def _():
             arrived(out1, 1)
             forward(out1, 1, t_in).start()
@@ -314,12 +311,12 @@
             arrived(in2, 0)
             forward(in2, 0, t_out).start()
 
-        @pl.when(~end & (k == 5))
+        @pl.when(~end & (k == 3))
         def _():
             arrived(in2, 1)
             forward(in2, 1, t_out).start()
 
-        @pl.when(~end & (k == 7))
+        @pl.when(~end & (k == 4))
         def _():
             arrived(in1, 1)
             forward(in1, 1, t_out).start()
@@ -327,21 +324,21 @@
 
     def dispatch_copy(m, d):
         return pltpu.make_async_remote_copy(
-            src_ref=disp.at[m, plane_peer(d)],
+            src_ref=disp.at[m, peers[d]],
             dst_ref=recv.at[m, j],
             send_sem=xs.at[m],
             recv_sem=xr.at[m],
-            device_id={"tile": plane_peer(d) * ZN + z},
+            device_id={"tile": peers[d] * ZN + z},
             device_id_type=MESH,
         )
 
     def return_copy(m, d):
         return pltpu.make_async_remote_copy(
-            src_ref=eout.at[m, plane_peer(d)],
+            src_ref=eout.at[m, peers[d]],
             dst_ref=ret.at[m, j],
             send_sem=ys.at[m],
             recv_sem=yr.at[m],
-            device_id={"tile": plane_peer(d) * ZN + z},
+            device_id={"tile": peers[d] * ZN + z},
             device_id_type=MESH,
         )
 
@@ -372,11 +369,8 @@
         picked = jnp.dot(table, x_all[s, part], preferred_element_type=f32)
         disp[m] = picked.reshape(JN, CAP, model).astype(bf16)
 
-        def start(d, carry):
+        for d in range(1, JN):
             dispatch_copy(m, d).start()
-            return carry
-
-        lax.fori_loop(1, JN, start, 0)
         recv[m, j] = disp[m, j]
 
     def stage_expert(m):
@@ -388,11 +382,8 @@
         result = jnp.dot(hidden, wd[...], preferred_element_type=f32)
         eout[m] = result.reshape(JN, CAP, model).astype(bf16)
 
-        def start(d, carry):
+        for d in range(1, JN):
             return_copy(m, d).start()
-            return carry
-
-        lax.fori_loop(1, JN, start, 0)
         ret[m, j] = eout[m, j]
 
     def sum_copy(m, dst, recv_sem, to):
@@ -504,6 +495,8 @@
         @pl.when(k < PIECES)
         def _():
             stage_dispatch(k)
+
+        pass_on(k)
 
         @pl.when((k >= 1) & (k < PIECES + 1))
         def _():

time: 120 us -> 105 us (0.88)
  Pallas kernels: 117 us -> 103 us
    pallas_call x1, Pallas kernels: 117 us -> 103 us  [local(): pl.pallas_call(layer_kernel, out_shape=jax.ShapeDtypeStruct((rows, model)...]
where the time goes in v5:
time: 105 us
  Pallas kernels  103 us (98%)
  local copies, waits for them, and re-layouts  1.87 us (2%)
    pallas_call x1, Pallas kernels, local(): pl.pallas_call(layer_kernel, out_shape=jax.ShapeDtypeStruct((rows, model)...  103 us

profile of v5, /device:TPU:64, one launch (start us, length us, event | category | flops | bytes accessed | tf_op | source)
XLA Modules:
  0.0 104.9 jit_solution(42698530745030597)
XLA Ops:
  0.0 103.0 %shard_map.109 = bf16[256,1024]{1,0:T(8,128)(2,1)} custom-call(bf16[256,1024]{1,0:T(8,128)(2,1)} %x_hbm.1, bf16[256,1024]{1,0:T(8,128)(2,1)} %q_hbm.1, bf16[256,1024]{1,0:T(8,128)(2,1)} %k_hbm.1, bf16[256,1024]{1,0:T(8,128)(2,1)} %v_hbm.1, bf16[1024,1024]{1,0:T(8,128)(2,1)} %ow_hbm.1, f32[1,1024]{1,0:T(1,128)} %bitcast.3, s32[2,256]{1,0:T(2,128)} %bitcast.4, ...), custom_call_target="tpu_custom_call" | custom-call | tf_op jit(solution)/shard_map/pallas_call | solution.py:591
  103.0 1.9 %copy.13 = bf16[256,1024]{1,0:T(8,128)(2,1)} copy(bf16[256,1024]{1,0:T(8,128)(2,1)} %shard_map.109) | data formatting | bytes 1048576
